TPU v7x, 768 devices: a whole 4x8x12 slice. The times are simulated.
768 devices in a mesh: sim: 32 (over z_hi, y, core), section: 24 (over x, z_lo).
Axes of the slice: x: 4, y: 8, z: 12 (z_hi: 2, z_lo: 6; z = z_hi * 6 + z_lo), core: 2. Of those that a mesh axis runs over, the one named last changes fastest.
Arguments:
- density: float32 [4, 3072, 3072], P(None, 'sim', 'section'), may hold values from 0.5 to 2
- momentum: float32 [3, 4, 3072, 3072], P(None, None, 'sim', 'section'), may hold values from -1 to 1
- energy: float32 [4, 3072, 3072], P(None, 'sim', 'section'), may hold values from 4 to 8
- membership: int32 [768, 768], P(('sim', 'section')), may hold values from 0 to 1535
- slot_of_brick: int32 [32, 24], P('sim'), may hold values from 0 to 23, each once within a row
Outputs:
- coded: float32 [5, 4, 3072, 3072], P(None, None, ('sim', 'section'))
- group_peak: float32 [5, 1536], replicated
Inputs may be any that keep to these rules, and one draw needn't show every extreme that they name: `slot_of_brick`: each row is a permutation of the 24 bricks.
All inputs are finite; a program needn't handle non-finite values.
Results may differ from a plain program's by a relative error of at most 0.0003.
Values sent between devices are 32-bit elements; how exact they have to be, the bound alone decides.
A program may use at most 32 MiB of HBM per device.

v0:
```python
import jax
import jax.numpy as jnp
from jax import lax
from jax.sharding import PartitionSpec as P

GAMMA_LESS = 0.4
COURANT = 0.05
DIFFUSE = 0.1
EPSILON = 1e-06
HIGH = lax.Precision.HIGHEST


def with_halo(block, sides, width):
    for axis, dim in sides:
        count = lax.axis_size(axis)
        forward = [(i, i + 1) for i in range(count - 1)]
        forward.append((count - 1, 0))
        backward = [(target, source) for source, target in forward]
        low = lax.ppermute(
            lax.slice_in_dim(block, block.shape[dim] - width, None, axis=dim), axis, forward
        )
        high = lax.ppermute(lax.slice_in_dim(block, 0, width, axis=dim), axis, backward)
        block = jnp.concatenate([low, block, high], axis=dim)
    return block


def flux_update(padded):
    density_c = padded[0]
    momentum_x = padded[1]
    momentum_y = padded[2]
    momentum_z = padded[3]
    energy_c = padded[4]
    velocity_x = momentum_x / density_c
    velocity_y = momentum_y / density_c
    kinetic = (
        0.5
        * (momentum_x * momentum_x + momentum_y * momentum_y + momentum_z * momentum_z)
        / density_c
    )
    pressure = GAMMA_LESS * (energy_c - kinetic)
    flux_x = jnp.stack(
        [
            momentum_x,
            momentum_x * velocity_x + pressure,
            momentum_y * velocity_x,
            momentum_z * velocity_x,
            (energy_c + pressure) * velocity_x,
        ]
    )
    flux_y = jnp.stack(
        [
            momentum_y,
            momentum_x * velocity_y,
            momentum_y * velocity_y + pressure,
            momentum_z * velocity_y,
            (energy_c + pressure) * velocity_y,
        ]
    )
    center = padded[:, :, 1:-1, 1:-1]
    spread = (
        padded[:, :, 1:-1, 2:]
        + padded[:, :, 1:-1, :-2]
        + padded[:, :, 2:, 1:-1]
        + padded[:, :, :-2, 1:-1]
        - 4.0 * center
    )
    return (
        center
        - COURANT * (flux_x[:, :, 1:-1, 2:] - flux_x[:, :, 1:-1, :-2])
        - COURANT * (flux_y[:, :, 2:, 1:-1] - flux_y[:, :, :-2, 1:-1])
        + DIFFUSE * spread
    )


def predict(extended):
    h = extended.shape[2] - 6
    guess = (
        -extended[:, :, 0:h]
        + 9.0 * extended[:, :, 2 : h + 2]
        + 9.0 * extended[:, :, 4 : h + 4]
        - extended[:, :, 6 : h + 6]
    ) / 16.0
    return extended[:, :, 3 : h + 3] - guess


def cosine_entry(k, d):
    factor = jnp.where(k == 0, 0.5, jnp.sqrt(0.5))
    return factor * jnp.cos(jnp.pi * (2.0 * d + 1.0) * k / 8.0)


def cosines():
    k = jnp.arange(4, dtype=jnp.float32)[:, None]
    m = jnp.arange(4, dtype=jnp.float32)[None, :]
    return cosine_entry(k, m)


def brick_matrix(brick_width):
    quarter = brick_width // 4
    m = jnp.arange(brick_width, dtype=jnp.int32)[:, None]
    column = jnp.arange(brick_width, dtype=jnp.int32)[None, :]
    k = column // quarter
    j = column % quarter
    d = m - 4 * j
    entries = cosine_entry(k.astype(jnp.float32), jnp.clip(d, 0, 3).astype(jnp.float32))
    return jnp.where((d >= 0) & (d < 4), entries, 0.0)


def transform(residual, brick_width):
    f, z, y, x = residual.shape
    along_z = jnp.einsum("kz,fzyx->fkyx", cosines(), residual, precision=HIGH)
    blocked = along_z.reshape(f, z, y // 4, 4, x)
    along_y = jnp.einsum("km,fzbmx->fzbkx", cosines(), blocked, precision=HIGH).reshape(f, z, y, x)
    bricks = along_y.reshape(f, z, y, x // brick_width, brick_width)
    return jnp.einsum("fzybm,mc->fzybc", bricks, brick_matrix(brick_width), precision=HIGH).reshape(
        f, z, y, x
    )


def reorder(coefficients, slot_of_brick, brick_width):
    f, z, y, x = coefficients.shape
    count = x // brick_width
    slabs = slot_of_brick.shape[0]
    placing = (
        slot_of_brick[:, :, None] == jnp.arange(count, dtype=jnp.int32)[None, None, :]
    ).astype(jnp.float32)
    bricks = coefficients.reshape(f, z, slabs, y // slabs, count, brick_width)
    return jnp.einsum("sbp,fzsybx->fzsypx", placing, bricks, precision=HIGH).reshape(f, z, y, x)


def block_peaks(coefficients, brick_width):
    f, z, y, x = coefficients.shape
    magnitude = jnp.max(jnp.abs(coefficients), axis=1)
    magnitude = jnp.max(magnitude.reshape(f, y // 4, 4, x), axis=2)
    magnitude = magnitude.reshape(f, y // 4, x // brick_width, 4, brick_width // 4)
    return jnp.max(magnitude, axis=3).reshape(f, y // 4, x // 4)


def gather_peaks(peaks, membership, groups):
    labels = jnp.arange(groups, dtype=jnp.int32)

    def gather_visit(carry, row):
        row_peaks, row_labels = row
        matches = row_labels[:, None] == labels[None, :]
        found = jnp.max(jnp.where(matches[None], row_peaks[:, :, None], 0.0), axis=1)
        return (jnp.maximum(carry, found), None)

    start = jnp.zeros((peaks.shape[0], groups), jnp.float32)
    result, unused = lax.scan(gather_visit, start, (jnp.moveaxis(peaks, 1, 0), membership))
    return result


def spread_peaks(group_peak, membership):
    labels = jnp.arange(group_peak.shape[1], dtype=jnp.int32)

    def spread_visit(row_labels):
        matches = (row_labels[:, None] == labels[None, :]).astype(jnp.float32)
        return jnp.dot(group_peak, matches.T, precision=HIGH)

    return jnp.moveaxis(lax.map(spread_visit, membership), 0, 1)


def normalize(coefficients, divisor, brick_width):
    f, z, y, x = coefficients.shape
    rows_count = y // 4
    widened = divisor.reshape(f, rows_count, x // brick_width, 1, brick_width // 4)
    widened = jnp.broadcast_to(
        widened, (f, rows_count, x // brick_width, 4, brick_width // 4)
    ).reshape(f, rows_count, x)
    widened = jnp.broadcast_to(widened[:, None, :, None, :], (f, z, rows_count, 4, x)).reshape(
        f, z, y, x
    )
    return coefficients / (widened + EPSILON)


def relay_slabs(blocks):
    return lax.all_to_all(blocks, "section", split_axis=2, concat_axis=3, tiled=True)


def shallow_update(conserved):
    padded = with_halo(conserved, (("sim", 2), ("section", 3)), 1)
    return flux_update(padded)


def per_device(density, momentum, energy, membership, slot_of_brick):
    conserved = jnp.concatenate([density[None], momentum, energy[None]], axis=0)
    brick_width = conserved.shape[3]
    updated = shallow_update(conserved)
    relayed = relay_slabs(updated)
    extended = with_halo(relayed, ((("sim", "section"), 2),), 3)
    transformed = transform(predict(extended), brick_width)
    placed = reorder(transformed, slot_of_brick, brick_width)
    peaks = block_peaks(placed, brick_width)
    groups = 2 * lax.axis_size("sim") * lax.axis_size("section")
    local_peak = gather_peaks(peaks, membership, groups)
    group_peak = lax.pmax(local_peak, ("sim", "section"))
    coded = normalize(placed, spread_peaks(group_peak, membership), brick_width)
    return (coded, group_peak)


def solution(mesh):
    placed = (
        P(None, "sim", "section"),
        P(None, None, "sim", "section"),
        P(None, "sim", "section"),
        P(("sim", "section"), None),
        P("sim", None),
    )
    return jax.shard_map(
        per_device,
        mesh=mesh,
        in_specs=placed,
        out_specs=(P(None, None, ("sim", "section"), None), P()),
        check_vma=False,
    )
```

profile of v0, /device:TPU:1, one launch (start us, length us, event | category | flops | bytes accessed | tf_op | source)
XLA Modules:
  0.0 275.0 jit_solution(11719773785667504885)
XLA Ops:
  0.6 1.3 pad_maximum_fusion.9
  1.9 4.6 %collective-permute-start = (f32[5,4,1,128]{3,0,2,1:T(8,128)S(1)}, f32[5,4,1,128]{3,0,2,1:T(8,128)S(1)}, u32[]{:S(2)}, u32[]{:S(2)}) collective-permute-start(f32[5,4,1,128]{3,0,2,1:T(8,128)S(1)} %copy.80), channel_id=1, source_target_pairs={{0,24},{24,48},{48,72},{72,96},{96,120},{120,144},{144,168},{168,1... | collective-permute-start | bytes 30728 | tf_op jit(solution)/shard_map/ppermute | solution.py:19
  6.5 9.7 %collective-permute-start.1 = (f32[5,4,1,128]{3,0,2,1:T(8,128)S(1)}, f32[5,4,1,128]{3,0,2,1:T(8,128)S(1)}, u32[]{:S(2)}, u32[]{:S(2)}) collective-permute-start(f32[5,4,1,128]{3,0,2,1:T(8,128)S(1)} %copy.81), channel_id=1, source_target_pairs={{24,0},{48,24},{72,48},{96,72},{120,96},{144,120},{168,144},{192,1... | collective-permute-start | bytes 30728 | tf_op jit(solution)/shard_map/ppermute | solution.py:22
  16.3 0.4 copy.64
  16.7 0.0 collective-permute-done
  16.7 0.4 copy.57
  17.1 0.0 collective-permute-done.1
  17.2 1.5 copy.59
  18.7 0.0 copy-start
  18.7 1.2 pad_maximum_fusion.10
  19.9 1.9 collective-permute-start.2
  21.8 10.3 %collective-permute-start.3 = (f32[5,4,98,1]{2,0,3,1:T(8,128)S(1)}, f32[5,4,98,1]{2,0,3,1:T(8,128)S(1)}, u32[]{:S(2)}, u32[]{:S(2)}) collective-permute-start(f32[5,4,98,1]{2,0,3,1:T(8,128)S(1)} %copy.61), channel_id=1, source_target_pairs={{1,0},{2,1},{3,2},{4,3},{5,4},{6,5},{7,6},{8,7},{9,8},{10,9},{11,1... | collective-permute-start | bytes 23528 | tf_op jit(solution)/shard_map/ppermute | solution.py:22
  32.1 0.0 collective-permute-done.2
  32.1 0.8 collective-permute-done.3
  33.0 0.0 copy-done
  33.0 0.8 pad_maximum_fusion
  33.8 0.1 add_dynamic-update-slice_fusion.1
  34.0 0.1 multiply_dynamic-update-slice_fusion.4
  34.1 0.1 multiply_dynamic-update-slice_fusion.2
  34.1 0.1 multiply_dynamic-update-slice_fusion.3
  34.3 0.1 multiply_dynamic-update-slice_fusion
  34.3 4.8 %fusion.3 = f32[5,4,96,128]{2,3,1,0:T(8,128)} fusion(f32[5,4,96,128]{2,3,1,0:T(8,128)S(1)} %copy.64, f32[5,4,1,128]{2,3,1,0:T(8,128)S(1)} %copy.57, f32[5,4,1,128]{2,3,1,0:T(8,128)S(1)} %copy-done, f32[5,4,98,1]{2,3,1,0:T(1,128)S(1)} %copy.62, f32[5,4,98,1]{2,3,1,0:T(1,128)S(1)} %copy.63, f32[5,4,98,130]{2,3,1,0:T(8,128)S(1)} %multiply_dynamic-update-slice_fusion, ...), kind=kLoop, calls=%fused_computation.10 | loop fusion | flops 5160960 | bytes 5934400 | tf_op jit(solution)/shard_map/add | solution.py:68
  39.2 2.7 copy.72
  41.9 59.0 %all_to_all.18 = f32[5,4,96,128]{3,0,1,2:T(8,128)S(1)} all-to-all(f32[5,4,96,128]{3,0,1,2:T(8,128)S(1)} %copy.72), channel_id=1, replica_groups=mesh['sim'=32,'section'=24] {'section'}, dimensions={2} | all-to-all | bytes 1966080 | tf_op jit(solution)/shard_map/all_to_all | solution.py:176
  100.9 0.6 copy.73
  101.5 0.3 all_to_all.16
  101.9 0.0 copy-start.2
  101.9 1.1 fusion.70
  103.0 2.2 collective-permute-start.4
  105.2 0.0 copy-done.2
  105.3 0.7 iota_compare_fusion
  106.0 14.4 %collective-permute-start.5 = (f32[5,4,3,3072]{3,1,2,0:T(4,128)S(1)}, f32[5,4,3,3072]{3,1,2,0:T(4,128)S(1)}, u32[]{:S(2)}, u32[]{:S(2)}) collective-permute-start(f32[5,4,3,3072]{3,1,2,0:T(4,128)S(1)} %get-tuple-element.46), channel_id=1, source_target_pairs={{1,0},{2,1},{3,2},{4,3},{5,4},{6,5},{7,6},{8,7},{9,8},{10,9},{11,1... | collective-permute-start | bytes 2211848 | tf_op jit(solution)/shard_map/ppermute | solution.py:22
  120.4 14.9 %collective-permute-done.4 = f32[5,4,3,3072]{3,1,2,0:T(4,128)} collective-permute-done((f32[5,4,3,3072]{3,1,2,0:T(4,128)}, f32[5,4,3,3072]{3,1,2,0:T(4,128)}, u32[]{:S(2)}, u32[]{:S(2)}) %collective-permute-start.4) | collective-permute-done | bytes 737312 | tf_op jit(solution)/shard_map/ppermute | solution.py:19
  135.3 1.2 constant_dynamic-update-slice_fusion.1
  136.4 0.3 constant_dynamic-update-slice_fusion
  136.8 1.3 collective-permute-done.5
  138.1 0.1 constant_dynamic-update-slice_fusion.2
  138.2 2.4 convolution_bitcast_fusion.1
  140.6 2.4 convolution_bitcast_fusion
  143.0 0.4 reshape_reshape.4
  143.4 0.0 copy-start.3
  143.4 1.2 fusion.20
  144.6 0.0 copy-done.3
  144.6 0.6 abs_reduce_fusion
  145.2 0.2 reshape.175
  145.3 0.2 reduce_max.33
  145.5 0.1 broadcast_in_dim.101
  145.6 2.2 select_reduce_fusion
  147.8 123.1 %pmax.7 = f32[5,1536]{1,0:T(8,128)S(1)} all-reduce(f32[5,1536]{1,0:T(8,128)S(1)} %broadcast_maximum_fusion), channel_id=1, replica_groups=mesh['sim'=32,'section'=24] {'sim','section'}, use_global_device_ids=true, to_apply=%region_3.4 | all-reduce | flops 7680 | bytes 61440 | tf_op jit(solution)/shard_map/pmax | solution.py:195
  270.8 0.0 copy-start.1
  270.8 2.2 convolution_add_fusion
  273.1 0.1 add.118
  273.2 0.2 add.119
  273.4 0.3 reshape.174
  273.8 0.0 copy-done.1
  273.8 1.2 broadcast_divide_fusion
  (16 shorter events, 0.2 us)
Async XLA Ops:
  1.9 14.7 %collective-permute-start = (f32[5,4,1,128]{3,0,2,1:T(8,128)S(1)}, f32[5,4,1,128]{3,0,2,1:T(8,128)S(1)}, u32[]{:S(2)}, u32[]{:S(2)}) collective-permute-start(f32[5,4,1,128]{3,0,2,1:T(8,128)S(1)} %copy.80), channel_id=1, source_target_pairs={{0,24},{24,48},{48,72},{72,96},{96,120},{120,144},{144,168},{168,1... | collective-permute-start | bytes 30728 | tf_op jit(solution)/shard_map/ppermute | solution.py:19
  6.5 10.6 %collective-permute-start.1 = (f32[5,4,1,128]{3,0,2,1:T(8,128)S(1)}, f32[5,4,1,128]{3,0,2,1:T(8,128)S(1)}, u32[]{:S(2)}, u32[]{:S(2)}) collective-permute-start(f32[5,4,1,128]{3,0,2,1:T(8,128)S(1)} %copy.81), channel_id=1, source_target_pairs={{24,0},{48,24},{72,48},{96,72},{120,96},{144,120},{168,144},{192,1... | collective-permute-start | bytes 30728 | tf_op jit(solution)/shard_map/ppermute | solution.py:22
  18.7 14.3 %copy-start = (f32[5,4,1,128]{2,3,1,0:T(8,128)S(1)}, f32[5,4,1,128]{2,3,1,0:T(8,128)}, u32[]{:S(2)}) copy-start(f32[5,4,1,128]{2,3,1,0:T(8,128)} %copy.59) | copy-start | bytes 30724
  19.9 12.2 %collective-permute-start.2 = (f32[5,4,98,1]{2,0,3,1:T(8,128)S(1)}, f32[5,4,98,1]{2,0,3,1:T(8,128)S(1)}, u32[]{:S(2)}, u32[]{:S(2)}) collective-permute-start(f32[5,4,98,1]{2,0,3,1:T(8,128)S(1)} %copy.60), channel_id=1, source_target_pairs={{0,1},{1,2},{2,3},{3,4},{4,5},{5,6},{6,7},{7,8},{8,9},{9,10},{10,1... | collective-permute-start | bytes 23528 | tf_op jit(solution)/shard_map/ppermute | solution.py:19
  21.8 11.1 %collective-permute-start.3 = (f32[5,4,98,1]{2,0,3,1:T(8,128)S(1)}, f32[5,4,98,1]{2,0,3,1:T(8,128)S(1)}, u32[]{:S(2)}, u32[]{:S(2)}) collective-permute-start(f32[5,4,98,1]{2,0,3,1:T(8,128)S(1)} %copy.61), channel_id=1, source_target_pairs={{1,0},{2,1},{3,2},{4,3},{5,4},{6,5},{7,6},{8,7},{9,8},{10,9},{11,1... | collective-permute-start | bytes 23528 | tf_op jit(solution)/shard_map/ppermute | solution.py:22
  101.9 3.4 %copy-start.2 = (s32[1,768]{1,0:T(1,128)S(1)}, s32[1,768]{1,0:T(1,128)}, u32[]{:S(2)}) copy-start(s32[1,768]{1,0:T(1,128)} %param.8) | copy-start | bytes 9220
  103.0 32.2 %collective-permute-start.4 = (f32[5,4,3,3072]{3,1,2,0:T(4,128)}, f32[5,4,3,3072]{3,1,2,0:T(4,128)}, u32[]{:S(2)}, u32[]{:S(2)}) collective-permute-start(f32[5,4,3,3072]{3,1,2,0:T(4,128)} %get-tuple-element.45), channel_id=1, source_target_pairs={{0,1},{1,2},{2,3},{3,4},{4,5},{5,6},{6,7},{7,8},{8,9},{9,10},{10,1... | collective-permute-start | bytes 2211848 | tf_op jit(solution)/shard_map/ppermute | solution.py:19
  106.0 32.1 %collective-permute-start.5 = (f32[5,4,3,3072]{3,1,2,0:T(4,128)S(1)}, f32[5,4,3,3072]{3,1,2,0:T(4,128)S(1)}, u32[]{:S(2)}, u32[]{:S(2)}) collective-permute-start(f32[5,4,3,3072]{3,1,2,0:T(4,128)S(1)} %get-tuple-element.46), channel_id=1, source_target_pairs={{1,0},{2,1},{3,2},{4,3},{5,4},{6,5},{7,6},{8,7},{9,8},{10,9},{11,1... | collective-permute-start | bytes 2211848 | tf_op jit(solution)/shard_map/ppermute | solution.py:22
  143.4 1.2 copy-start.3
  270.8 2.9 %copy-start.1 = (f32[5,1536]{1,0:T(8,128)}, f32[5,1536]{1,0:T(8,128)S(1)}, u32[]{:S(2)}) copy-start(f32[5,1536]{1,0:T(8,128)S(1)} %pmax.7) | copy-start | bytes 92164
where the time goes:
time: 275 us
  blocking collectives  182 us (66%)
  starting transfers between devices  43 us (16%)
  waiting for transfers between devices  17 us (6%)
  other arithmetic  12.9 us (5%)
  local copies, waits for them, and re-layouts  10.1 us (4%)
  matrix products  8.78 us (3%)
    pmax x1, blocking collectives, per_device(): group_peak = lax.pmax(local_peak, ('sim', 'section'))  123 us
    all_to_all x1, blocking collectives, relay_slabs(): lax.all_to_all(blocks, 'section', split_axis=2, concat_axis=3, tiled=True)  59 us
    ppermute x3, starting transfers between devices, with_halo(): lax.ppermute(lax.slice_in_dim(block, 0, width, axis=dim), axis, backward)  34.4 us
    ppermute x3, waiting for transfers between devices, with_halo(): lax.ppermute(lax.slice_in_dim(block, block.shape[dim] - width, None, axis...  14.9 us
    ppermute x3, starting transfers between devices, with_halo(): lax.ppermute(lax.slice_in_dim(block, block.shape[dim] - width, None, axis...  8.67 us
  transfers between devices with their start and end apart: 6, of which 3 were waited for; matrix products, arithmetic and copies ran while one was open for 1% of the time, Pallas kernels for 0%

commit v1 on v0

v1 whole, which is shorter than its diff:
```python
import functools

import jax
import jax.numpy as jnp
import numpy as np
from jax import lax
from jax.experimental import pallas as pl
from jax.experimental.pallas import tpu as pltpu
from jax.sharding import PartitionSpec as P

Z_HI, Y_CHIPS, CORES = 2, 8, 2
X_CHIPS, Z_LO = 4, 6
GAMMA_LESS, COURANT, DIFFUSE, EPSILON = 0.4, 0.05, 0.1, 1e-06
FIELDS, PLANES, LANES, EDGE = 5, 4, 128, 8
GROUPS = 1536
HIGH = lax.Precision.HIGHEST
MESH = pl.DeviceIdType.MESH


def cosines():
    k = np.arange(4)[:, None]
    m = np.arange(4)[None, :]
    return np.where(k == 0, 0.5, np.sqrt(0.5)) * np.cos(np.pi * (2 * m + 1) * k / 8)


def row_matrix(rows):
    predict = np.zeros((rows, rows + 2 * EDGE))
    for y in range(rows):
        at = y + EDGE
        predict[y, at] = 1.0
        predict[y, [at - 1, at + 1]] = -9.0 / 16.0
        predict[y, [at - 3, at + 3]] = 1.0 / 16.0
    return (np.kron(np.eye(rows // 4), cosines()) @ predict).astype(np.float32)


def brick_matrix():
    c = cosines()
    out = np.zeros((LANES, LANES))
    for j in range(LANES // 4):
        for k in range(4):
            out[4 * j : 4 * j + 4, k * (LANES // 4) + j] = c[k]
    return out.astype(np.float32)


def state_terms(c):
    rho, mx, my, mz, energy = c
    inverse = 1.0 / rho
    u = mx * inverse
    v = my * inverse
    pressure = GAMMA_LESS * (energy - 0.5 * (mx * mx + my * my + mz * mz) * inverse)
    total = energy + pressure
    flux_x = (mx, mx * u + pressure, my * u, mz * u, total * u)
    flux_y = (my, mx * v, my * v + pressure, mz * v, total * v)
    spread = [DIFFUSE * a for a in c]
    return (
        [b - COURANT * a for a, b in zip(flux_x, spread)],
        [b + COURANT * a for a, b in zip(flux_x, spread)],
        [b - COURANT * a for a, b in zip(flux_y, spread)],
        [b + COURANT * a for a, b in zip(flux_y, spread)],
    )


def step_kernel(
    slot_ref,
    density,
    momentum,
    energy,
    members,
    rows_ref,
    brick_ref,
    landed,
    final,
    ext,
    center,
    from_above,
    from_below,
    outbox,
    folded,
    member_rows,
    member_cols,
    edge_out,
    edge_in,
    edge_term,
    best,
    own,
    pass1,
    pass2,
    pass3,
    hold,
    full,
    load_sem,
    row_send,
    row_recv,
    edge_send,
    edge_recv,
    member_send,
    member_recv,
    bulk_send,
    bulk_recv,
    own_sem,
    red_send,
    red_recv,
):
    n_section = X_CHIPS * Z_LO
    n_sim = Z_HI * Y_CHIPS * CORES
    rows = 4 * n_section
    tiles = rows // 8
    s = lax.axis_index("sim")
    t = lax.axis_index("section")
    core = s % CORES
    y = (s // CORES) % Y_CHIPS
    z_hi = s // (CORES * Y_CHIPS)
    x = t // Z_LO
    z_lo = t % Z_LO
    below, above = (s + n_sim - 1) % n_sim, (s + 1) % n_sim
    left, right = (t + n_section - 1) % n_section, (t + 1) % n_section
    lane = lax.broadcasted_iota(jnp.int32, (8, LANES), 1)

    loads = [
        pltpu.make_async_copy(density, ext.at[0, :, pl.ds(EDGE, rows), :], load_sem.at[0]),
        pltpu.make_async_copy(momentum, ext.at[pl.ds(1, 3), :, pl.ds(EDGE, rows), :], load_sem.at[1]),
        pltpu.make_async_copy(energy, ext.at[4, :, pl.ds(EDGE, rows), :], load_sem.at[2]),
        pltpu.make_async_copy(members, member_rows.at[t], load_sem.at[3]),
    ]
    for copy in loads:
        copy.start()

    barrier = pltpu.get_barrier_semaphore()
    shards = CORES * X_CHIPS
    place = core * X_CHIPS + x
    z_all = Z_HI * Z_LO
    z = z_hi * Z_LO + z_lo

    def in_plane(step):
        other = (place + step) % shards
        return (s - core + other // X_CHIPS, (other % X_CHIPS) * Z_LO + z_lo)

    def in_column(step):
        return (s + ((y + step) % Y_CHIPS - y) * CORES, t)

    def in_depth(step):
        other = (z + step) % z_all
        return (s + (other // Z_LO - z_hi) * (CORES * Y_CHIPS), x * Z_LO + other % Z_LO)

    def greet(device):
        pl.semaphore_signal(barrier, inc=1, device_id=device, device_id_type=MESH)

    def greet_section(d, carry):
        greet((s, (t + d) % n_section))
        return carry

    lax.fori_loop(1, n_section, greet_section, 0)
    for sim in (below, above):
        for section in (left, t, right):
            greet((sim, section))
    for d in range(1, X_CHIPS):
        greet((s + 1 - 2 * core, ((x + d) % X_CHIPS) * Z_LO + z_lo))
    for d in range(1, Y_CHIPS):
        greet(in_column(d))
    if Z_HI > 1:
        for d in range(Z_LO):
            greet(((s + n_sim // 2) % n_sim, x * Z_LO + d))
    greetings = (n_section - 1) + 6 + (X_CHIPS - 1) + (Y_CHIPS - 1) + (Z_LO if Z_HI > 1 else 0)

    for copy in loads:
        copy.wait()

    def pack(f, carry):
        low = jnp.zeros((8, LANES), jnp.float32)
        high = jnp.zeros((8, LANES), jnp.float32)
        for plane in range(PLANES):
            for r in range(tiles):
                value = ext[f, plane, pl.ds(EDGE + 8 * r, 8), :]
                at = 4 * r + plane
                low = jnp.where(lane == at, pltpu.roll(value, at, 1) if at else value, low)
                high = jnp.where(lane == 127 - at, pltpu.roll(value, 128 - at, 1) if at else value, high)
        edge_out[0, f] = low
        edge_out[1, f] = high
        return carry

    lax.fori_loop(0, FIELDS, pack, 0)

    def cells(plane, r):
        start = pl.multiple_of(8 * r, 8) if not isinstance(r, int) else 8 * r
        c = [ext[f, plane, pl.ds(start, 8), :] for f in range(FIELDS)]
        low_x, high_x, low_y, high_y = state_terms(c)
        for f in range(FIELDS):
            up = jnp.where(lane == LANES - 1, 0.0, pltpu.roll(low_x[f], LANES - 1, 1))
            down = jnp.where(lane == 0, 0.0, pltpu.roll(high_x[f], 1, 1))
            center[f, plane, pl.ds(start, 8), :] = (1.0 - 4.0 * DIFFUSE) * c[f] + up + down
            from_above[f, plane, pl.ds(start, 8), :] = low_y[f]
            from_below[f, plane, pl.ds(start, 8), :] = high_y[f]

    def inner(plane, carry):
        def visit(r, carry):
            cells(plane, r)
            return carry

        return lax.fori_loop(1, tiles + 1, visit, carry)

    lax.fori_loop(0, PLANES, inner, 0)

    pl.semaphore_wait(barrier, greetings)

    sends = []

    def send(source, target, send_sem, recv_sem, device):
        copy = pltpu.make_async_remote_copy(
            src_ref=source, dst_ref=target, send_sem=send_sem, recv_sem=recv_sem, device_id=device, device_id_type=MESH
        )
        copy.start()
        return copy

    def arrived(ref, sem):
        pltpu.make_async_copy(ref, ref, sem).wait()

    for side, step in ((0, left), (1, right)):
        for k, sim in ((0, above), (1, s), (2, below)):
            sends.append(send(edge_out.at[side], edge_in.at[1 - side, k], edge_send.at[side, k], edge_recv.at[1 - side, k], (sim, step)))
    for i, (first, to, sim) in enumerate(((0, EDGE + rows, below), (rows - 8, 0, above))):
        sends.append(send(density.at[:, pl.ds(first, 8), :], ext.at[0, :, pl.ds(to, 8), :], row_send.at[i, 0], row_recv.at[i, 0], (sim, t)))
        sends.append(send(momentum.at[:, :, pl.ds(first, 8), :], ext.at[pl.ds(1, 3), :, pl.ds(to, 8), :], row_send.at[i, 1], row_recv.at[i, 1], (sim, t)))
        sends.append(send(energy.at[:, pl.ds(first, 8), :], ext.at[4, :, pl.ds(to, 8), :], row_send.at[i, 2], row_recv.at[i, 2], (sim, t)))

    def send_members(d, carry):
        send(members, member_rows.at[t], member_send, member_recv, (s, (t + d) % n_section))
        return carry

    lax.fori_loop(1, n_section, send_members, 0)

    for copy in sends:
        copy.wait_recv()

    def edges(k, carry):
        for side in range(2):
            c = [edge_in[side, k, f] for f in range(FIELDS)]
            terms = state_terms(c)[1 - side]
            for f in range(FIELDS):
                edge_term[side, k, f] = terms[f]
        return carry

    lax.fori_loop(0, 3, edges, 0)

    def outer(plane, carry):
        cells(plane, 0)
        cells(plane, tiles + 1)
        return carry

    lax.fori_loop(0, PLANES, outer, 0)

    c = cosines()
    a1, b1 = float(c[1, 0]), float(c[1, 1])

    def transform(f, carry):
        parts = []
        for plane in range(PLANES):
            added = []
            for r in range(tiles + 2):
                k = 0 if r == 0 else 2 if r == tiles + 1 else 1
                at = 4 * ((r - 1) % tiles) + plane
                low = pltpu.roll(edge_term[0, k, f], at + 1, 1)
                high = edge_term[1, k, f] if at == 127 else pltpu.roll(edge_term[1, k, f], 127 - at, 1)
                added.append(jnp.where(lane == 0, low, jnp.where(lane == LANES - 1, high, 0.0)))
            height = rows + 2 * EDGE
            updated = center[f, plane] + jnp.concatenate(added, axis=0)
            updated += pltpu.roll(from_above[f, plane], height - 1, 0)
            updated += pltpu.roll(from_below[f, plane], 1, 0)
            parts.append(jnp.dot(rows_ref[...], updated, precision=HIGH, preferred_element_type=jnp.float32))
        outer_sum, inner_sum = parts[0] + parts[3], parts[1] + parts[2]
        outer_gap, inner_gap = parts[0] - parts[3], parts[1] - parts[2]
        mixed = jnp.concatenate(
            [
                0.5 * (outer_sum + inner_sum),
                a1 * outer_gap + b1 * inner_gap,
                0.5 * (outer_sum - inner_sum),
                b1 * outer_gap - a1 * inner_gap,
            ],
            axis=0,
        )
        done = jnp.dot(mixed, brick_ref[...], precision=HIGH, preferred_element_type=jnp.float32)
        peak = None
        for k in range(PLANES):
            plane = done[k * rows : (k + 1) * rows]
            outbox[:, f, k] = plane.reshape(n_section, 4, LANES)
            peak = jnp.abs(plane) if peak is None else jnp.maximum(peak, jnp.abs(plane))
        peak = jnp.maximum(peak, pltpu.roll(peak, 32, 1))
        peak = jnp.maximum(peak, pltpu.roll(peak, 64, 1))
        peak = jnp.maximum(peak, pltpu.roll(peak, rows - 1, 0))
        peak = jnp.maximum(peak, pltpu.roll(peak, rows - 2, 0))
        folded[f, pl.ds(0, rows), :] = peak

        def deliver(d, carry):
            to = (t + d) % n_section
            send(outbox.at[to, f], landed.at[t, f], bulk_send, bulk_recv, (s, to))
            return carry

        lax.fori_loop(1, n_section, deliver, 0)
        pltpu.make_async_copy(outbox.at[t, f], landed.at[t, f], own_sem).start()
        return carry

    lax.fori_loop(0, FIELDS, transform, 0)

    some = pl.ds(0, n_section - 1)
    arrived(member_rows.at[some], member_recv)
    block_rows = member_cols.shape[1]
    for r in range(n_section):
        for col in range(n_section // 4):
            member_cols[col, pl.ds(r, 1), :] = member_rows[r, :, pl.ds(col * LANES, LANES)]
    slots = slot_ref[...].astype(jnp.float32)
    at = lax.broadcasted_iota(jnp.int32, slots.shape, 1)
    slot = jnp.max(jnp.where(at == t, slots, 0.0), axis=1, keepdims=True)
    slot = jnp.broadcast_to(slot, (block_rows, LANES))
    labels = jnp.full((block_rows, LANES), -1, jnp.int32)
    for p in range(n_section):
        window = member_cols[p // 4]
        turned = pltpu.roll(window, LANES - 32 * (p % 4), 1) if p % 4 else window
        labels = jnp.where(slot == float(p), turned, labels)
    peaks = [folded[f, pl.ds(0, block_rows, stride=4), :] for f in range(FIELDS)]
    best[...] = jnp.zeros(best.shape, jnp.float32)
    columns = GROUPS // LANES
    wide = lax.broadcasted_iota(jnp.int32, (block_rows, LANES), 1)

    def collect(j, carry):
        labels, peaks = carry[0], carry[1:]
        label = jnp.broadcast_to(labels[:, 0:1], (block_rows, LANES))
        spread = [jnp.broadcast_to(p[:, 0:1], (block_rows, LANES)) for p in peaks]
        for col in range(columns):
            match = label == wide + LANES * col
            for f in range(FIELDS):
                found = jnp.where(match, spread[f], 0.0)
                top = best[f, col]
                for r in range(block_rows // 8):
                    top = jnp.maximum(top, found[8 * r : 8 * r + 8])
                best[f, col] = top
        return tuple(pltpu.roll(a, LANES - 1, 1) for a in carry)

    lax.fori_loop(0, 32, collect, (labels, *peaks))

    depth = own.shape[1]
    own[...] = jnp.zeros(own.shape, jnp.float32)
    for f in range(FIELDS):
        for col in range(columns):
            at = f * columns + col
            own[at // depth, pl.ds(at % depth, 1), :] = jnp.max(best[f, col], axis=0, keepdims=True)

    for d in range(1, shards):
        other = (place + d) % shards
        send(own.at[other], pass1.at[d - 1], red_send.at[0], red_recv.at[0], in_plane(d))
    arrived(pass1, red_recv.at[0])
    value = own[place]
    for d in range(shards - 1):
        value = jnp.maximum(value, pass1[d])
    if Y_CHIPS > 1:
        hold[0] = value
        for d in range(1, Y_CHIPS):
            send(hold.at[0], pass2.at[d - 1], red_send.at[1], red_recv.at[1], in_column(d))
        arrived(pass2, red_recv.at[1])
        for d in range(Y_CHIPS - 1):
            value = jnp.maximum(value, pass2[d])
    hold[1] = value
    for d in range(1, z_all):
        send(hold.at[1], pass3.at[d - 1], red_send.at[2], red_recv.at[2], in_depth(d))
    arrived(pass3, red_recv.at[2])
    for d in range(z_all - 1):
        value = jnp.maximum(value, pass3[d])
    hold[2] = value
    for d in range(1, shards):
        send(hold.at[2], full.at[place], red_send.at[3], red_recv.at[3], in_plane(d))
    full[place] = value
    arrived(full.at[pl.ds(0, shards - 1)], red_recv.at[3])
    for i in range(shards):
        final[pl.ds(i * depth, depth), :] = full[i]

    for copy in sends:
        copy.wait_send()
    arrived(member_rows.at[some], member_send)
    arrived(outbox.at[some], bulk_send)
    arrived(pass1, red_send.at[0])
    if Y_CHIPS > 1:
        arrived(pass2, red_send.at[1])
    arrived(pass3, red_send.at[2])
    arrived(pass1, red_send.at[3])
    arrived(landed.at[0], own_sem)
    arrived(landed.at[some], bulk_recv)


def place_kernel(slot_ref, final, members, landed, coded, group_peak, peaks, scale):
    n_section = landed.shape[0]
    columns = GROUPS // LANES

    @pl.when(pl.program_id(0) == 0)
    def _():
        peaks[...] = jnp.zeros(peaks.shape, jnp.float32)
        for f in range(FIELDS):
            for col in range(columns):
                peaks[f : f + 1, col * LANES : (col + 1) * LANES] = final[f * columns + col : f * columns + col + 1, :]
        group_peak[...] = peaks[0:FIELDS, :]
        lane = lax.broadcasted_iota(jnp.int32, (8, LANES), 1)
        for block in range(n_section // 4):
            label = jnp.broadcast_to(members[0:1, block * LANES : (block + 1) * LANES], (8, LANES))
            high, low = label // LANES, label % LANES
            found = jnp.zeros((8, LANES), jnp.float32)
            for col in range(columns):
                picked = jnp.take_along_axis(
                    peaks[:, col * LANES : (col + 1) * LANES], low, axis=1, mode="promise_in_bounds"
                )
                found = jnp.where(high == col, picked, found)
            found = found + EPSILON
            turned = [found] + [pltpu.roll(found, 32 * q, 1) for q in range(1, 4)]
            for q in range(4):
                full = turned[(0 - q) % 4]
                for a in range(1, 4):
                    full = jnp.where(lane // 32 == a, turned[(a - q) % 4], full)
                for f in range(FIELDS):
                    scale[f, 4 * block + q] = full[f : f + 1]

    f = pl.program_id(0)

    for b in range(n_section):
        slot = slot_ref[0, b]
        divisor = scale[f, slot]
        coded[0, :, :, pl.ds(pl.multiple_of(slot * LANES, LANES), LANES)] = landed[b, 0] / divisor[None]


def per_device(density, momentum, energy, membership, slot_of_brick):
    planes, rows, width = density.shape
    n_section = rows // 4
    block_rows = -(-n_section // 8) * 8
    shards = CORES * X_CHIPS
    depth = 64 // shards
    f32 = jnp.float32
    height = rows + 2 * EDGE
    vmem, anywhere = pl.BlockSpec(memory_space=pltpu.VMEM), pl.BlockSpec(memory_space=pl.ANY)
    smem = pl.BlockSpec(memory_space=pltpu.SMEM)
    dma = pltpu.SemaphoreType.DMA
    landed, final = pl.pallas_call(
        step_kernel,
        out_shape=(
            jax.ShapeDtypeStruct((n_section, FIELDS, planes, 4, width), f32),
            jax.ShapeDtypeStruct((64, width), f32),
        ),
        in_specs=[vmem, anywhere, anywhere, anywhere, anywhere, vmem, vmem],
        out_specs=(anywhere, vmem),
        scratch_shapes=[
            pltpu.VMEM((FIELDS, planes, height, width), f32),
            pltpu.VMEM((FIELDS, planes, height, width), f32),
            pltpu.VMEM((FIELDS, planes, height, width), f32),
            pltpu.VMEM((FIELDS, planes, height, width), f32),
            pltpu.VMEM((n_section, FIELDS, planes, 4, width), f32),
            pltpu.VMEM((FIELDS, 4 * block_rows, width), f32),
            pltpu.VMEM((n_section, 1, membership.shape[1]), jnp.int32),
            pltpu.VMEM((n_section // 4, block_rows, width), jnp.int32),
            pltpu.VMEM((2, FIELDS, 8, width), f32),
            pltpu.VMEM((2, 3, FIELDS, 8, width), f32),
            pltpu.VMEM((2, 3, FIELDS, 8, width), f32),
            pltpu.VMEM((FIELDS, GROUPS // width, 8, width), f32),
            pltpu.VMEM((shards, depth, width), f32),
            pltpu.VMEM((shards - 1, depth, width), f32),
            pltpu.VMEM((max(Y_CHIPS - 1, 1), depth, width), f32),
            pltpu.VMEM((Z_HI * Z_LO - 1, depth, width), f32),
            pltpu.VMEM((3, depth, width), f32),
            pltpu.VMEM((shards, depth, width), f32),
            dma((4,)),
            dma((2, 3)),
            dma((2, 3)),
            dma((2, 3)),
            dma((2, 3)),
            dma,
            dma,
            dma,
            dma,
            dma,
            dma((4,)),
            dma((4,)),
        ],
        compiler_params=pltpu.CompilerParams(collective_id=0, has_side_effects=True),
        name="step",
    )(slot_of_brick, density, momentum, energy, membership, row_matrix(rows), brick_matrix())
    return pl.pallas_call(
        place_kernel,
        grid=(FIELDS,),
        out_shape=(
            jax.ShapeDtypeStruct((FIELDS, planes, 4, n_section * width), f32),
            jax.ShapeDtypeStruct((FIELDS, GROUPS), f32),
        ),
        in_specs=[
            smem,
            pl.BlockSpec((64, width), lambda f: (0, 0)),
            pl.BlockSpec(membership.shape, lambda f: (0, 0)),
            pl.BlockSpec((n_section, 1, planes, 4, width), lambda f: (0, f, 0, 0, 0)),
        ],
        out_specs=(
            pl.BlockSpec((1, planes, 4, n_section * width), lambda f: (f, 0, 0, 0)),
            pl.BlockSpec((FIELDS, GROUPS), lambda f: (0, 0)),
        ),
        scratch_shapes=[pltpu.VMEM((8, GROUPS), f32), pltpu.VMEM((FIELDS, n_section, 1, width), f32)],
        name="place",
    )(slot_of_brick, final, membership, landed)


def solution(mesh):
    placed = (
        P(None, "sim", "section"),
        P(None, None, "sim", "section"),
        P(None, "sim", "section"),
        P(("sim", "section"), None),
        P("sim", None),
    )
    return jax.shard_map(
        per_device,
        mesh=mesh,
        in_specs=placed,
        out_specs=(P(None, None, ("sim", "section"), None), P()),
        check_vma=False,
    )
```

time: 275 us -> 75.1 us (0.27)
  blocking collectives: 182 us -> 0 us
  Pallas kernels: 0 us -> 74.2 us
  starting transfers between devices: 43 us -> 0 us
  waiting for transfers between devices: 17 us -> 0 us
  other arithmetic: 12.9 us -> 0 us
  local copies, waits for them, and re-layouts: 10.1 us -> 0 us
  matrix products: 8.78 us -> 0 us
    pmax x1 -> x0, blocking collectives: 123 us -> none  [per_device(): group_peak = lax.pmax(local_peak, ('sim', 'section'))]
    pallas_call x0 -> x2, Pallas kernels: none -> 74.2 us  [the longest x1 69.9 us: per_device(): pl.pallas_call(step_kernel, out_shape=(jax.ShapeDtypeStruct((n_section, F...]
    all_to_all x1 -> x0, blocking collectives: 59 us -> none  [relay_slabs(): lax.all_to_all(blocks, 'section', split_axis=2, concat_axis=3, tiled=True)]
    ppermute x6 -> x0, starting transfers between devices: 43 us -> none  [the longest x3 34.4 us: with_halo(): lax.ppermute(lax.slice_in_dim(block, 0, width, axis=dim), axis, backward)]
    ppermute x6 -> x0, waiting for transfers between devices: 17 us -> none  [the longest x3 14.9 us: with_halo(): lax.ppermute(lax.slice_in_dim(block, block.shape[dim] - width, None, axis...]
    dot_general x5 -> x0, matrix products: 8.78 us -> none  [the longest x1 2.42 us: transform(): along_z = jnp.einsum('kz,fzyx->fkyx', cosines(), residual, precision=HIGH)]
    add x1 -> x0, other arithmetic: 4.85 us -> none  [flux_update(): center - COURANT * (flux_x[:, :, 1:-1, 2:] - flux_x[:, :, 1:-1, :-2])]
    concatenate x3 -> x0, other arithmetic: 3.27 us -> none  [the longest x2 1.99 us: with_halo(): block = jnp.concatenate([low, block, high], axis=dim)]
  transfers between devices with their start and end apart: 6 -> 0, of which waited for: 3 -> 0; matrix products, arithmetic and copies ran while one was open for 1% -> 0% of each run, Pallas kernels for 0% -> 0%
where the time goes in v1:
time: 75.1 us; the launch traced here: 74.8 us
  Pallas kernels  74.2 us (99%)
    pallas_call x1, Pallas kernels, per_device(): pl.pallas_call(step_kernel, out_shape=(jax.ShapeDtypeStruct((n_section, F...  69.9 us
    pallas_call x1, Pallas kernels, per_device(): pl.pallas_call(place_kernel, grid=(FIELDS,), out_shape=(jax.ShapeDtypeStr...  4.28 us

profile of v1, /device:TPU:1, one launch (start us, length us, event | category | flops | bytes accessed | tf_op | source)
XLA Modules:
  0.0 74.8 jit_solution(13136389941875528965)
XLA Ops:
  0.6 69.9 %step.1 = (f32[24,5,4,4,128]{4,3,2,1,0:T(4,128)}, f32[64,128]{1,0:T(8,128)}) custom-call(s32[1,24]{1,0:T(1,128)} %slot_ref.3, f32[4,96,128]{2,1,0:T(8,128)} %density.1, f32[3,4,96,128]{3,2,1,0:T(8,128)} %momentum.1, f32[4,96,128]{2,1,0:T(8,128)} %energy.1, s32[1,768]{1,0:T(1,128)} %members.3, f32[96,112]{1,0:T(8,128)} %constant.4.clone.rows_ref, ...), custom_call_target="tpu_custom_call" | custom-call | tf_op jit(solution)/shard_map/step/pallas_call | solution.py:436
  70.5 4.3 %place.1 = (f32[5,4,4,3072]{3,2,1,0:T(4,128)}, f32[5,1536]{1,0:T(8,128)}) custom-call(s32[1,24]{1,0:T(1,128)} %slot_ref.3, f32[64,128]{1,0:T(8,128)} %get-tuple-element.4.final, s32[1,768]{1,0:T(1,128)} %members.3, f32[24,5,4,4,128]{4,3,2,1,0:T(4,128)} %get-tuple-element.5.landed), custom_call_target="tpu_custom_call" | custom-call | tf_op jit(solution)/shard_map/place/pallas_call | solution.py:479

commit v2 on v1

--- a/solution.py
+++ b/solution.py
@@ -40,6 +40,10 @@
         for k in range(4):
             out[4 * j : 4 * j + 4, k * (LANES // 4) + j] = c[k]
     return out.astype(np.float32)
+
+
+def depth_matrix():
+    return np.kron(np.eye(LANES // 4), cosines().T).astype(np.float32)
 
 
 def state_terms(c):
@@ -68,13 +72,18 @@
     members,
     rows_ref,
     brick_ref,
+    depth_ref,
     landed,
+    fringe,
     final,
     ext,
     center,
     from_above,
     from_below,
     outbox,
+    late,
+    edge_rows,
+    fringe_out,
     folded,
     member_rows,
     member_cols,
@@ -98,6 +107,9 @@
     bulk_send,
     bulk_recv,
     own_sem,
+    fringe_send,
+    fringe_recv,
+    fringe_own,
     red_send,
     red_recv,
 ):
@@ -190,82 +202,82 @@
             center[f, plane, pl.ds(start, 8), :] = (1.0 - 4.0 * DIFFUSE) * c[f] + up + down
             from_above[f, plane, pl.ds(start, 8), :] = low_y[f]
             from_below[f, plane, pl.ds(start, 8), :] = high_y[f]
-
-    def inner(plane, carry):
-        def visit(r, carry):
-            cells(plane, r)
-            return carry
-
-        return lax.fori_loop(1, tiles + 1, visit, carry)
-
-    lax.fori_loop(0, PLANES, inner, 0)
-
-    pl.semaphore_wait(barrier, greetings)
-
-    sends = []
+        return low_x, high_x
+
+    nothing = jnp.zeros((8, LANES), jnp.float32)
+    height = rows + 2 * EDGE
+    for first in (0, height - 8):
+        edge_rows[pl.ds(first, 8), :] = nothing
+        for f in range(FIELDS):
+            for plane in range(PLANES):
+                for ref in (center, from_above, from_below):
+                    ref[f, plane, pl.ds(first, 8), :] = nothing
+
+    def inner(r, carry):
+        packed = nothing
+        for plane in range(PLANES):
+            low_x, high_x = cells(plane, r)
+            for f in range(FIELDS):
+                at = PLANES * f + plane
+                packed = jnp.where(lane == at, pltpu.roll(low_x[f], at, 1) if at else low_x[f], packed)
+                packed = jnp.where(lane == 64 + at, pltpu.roll(high_x[f], 65 + at, 1), packed)
+        edge_rows[pl.ds(pl.multiple_of(8 * r, 8), 8), :] = packed
+        return carry
+
+    lax.fori_loop(1, tiles + 1, inner, 0)
+
+    def product(a, b):
+        return jnp.dot(a, b, precision=HIGH, preferred_element_type=jnp.float32)
+
+    edges_done = product(product(rows_ref[...], edge_rows[...]), depth_ref[...])
+    fringe_out[...] = edges_done.reshape(n_section, 4, LANES)
+    for first in (0, n_section - 1):
+        fringe_out[first] = jnp.zeros((4, LANES), jnp.float32)
 
     def send(source, target, send_sem, recv_sem, device):
         copy = pltpu.make_async_remote_copy(
             src_ref=source, dst_ref=target, send_sem=send_sem, recv_sem=recv_sem, device_id=device, device_id_type=MESH
         )
         copy.start()
-        return copy
 
     def arrived(ref, sem):
         pltpu.make_async_copy(ref, ref, sem).wait()
 
-    for side, step in ((0, left), (1, right)):
-        for k, sim in ((0, above), (1, s), (2, below)):
-            sends.append(send(edge_out.at[side], edge_in.at[1 - side, k], edge_send.at[side, k], edge_recv.at[1 - side, k], (sim, step)))
-    for i, (first, to, sim) in enumerate(((0, EDGE + rows, below), (rows - 8, 0, above))):
-        sends.append(send(density.at[:, pl.ds(first, 8), :], ext.at[0, :, pl.ds(to, 8), :], row_send.at[i, 0], row_recv.at[i, 0], (sim, t)))
-        sends.append(send(momentum.at[:, :, pl.ds(first, 8), :], ext.at[pl.ds(1, 3), :, pl.ds(to, 8), :], row_send.at[i, 1], row_recv.at[i, 1], (sim, t)))
-        sends.append(send(energy.at[:, pl.ds(first, 8), :], ext.at[4, :, pl.ds(to, 8), :], row_send.at[i, 2], row_recv.at[i, 2], (sim, t)))
-
-    def send_members(d, carry):
-        send(members, member_rows.at[t], member_send, member_recv, (s, (t + d) % n_section))
-        return carry
-
-    lax.fori_loop(1, n_section, send_members, 0)
-
-    for copy in sends:
-        copy.wait_recv()
-
-    def edges(k, carry):
-        for side in range(2):
-            c = [edge_in[side, k, f] for f in range(FIELDS)]
-            terms = state_terms(c)[1 - side]
-            for f in range(FIELDS):
-                edge_term[side, k, f] = terms[f]
-        return carry
-
-    lax.fori_loop(0, 3, edges, 0)
-
-    def outer(plane, carry):
-        cells(plane, 0)
-        cells(plane, tiles + 1)
-        return carry
-
-    lax.fori_loop(0, PLANES, outer, 0)
+    def halo_copies():
+        plan = []
+        for side, step in ((0, left), (1, right)):
+            for k, sim in ((0, above), (1, s), (2, below)):
+                plan.append((edge_out.at[side], edge_in.at[1 - side, k], edge_send.at[side, k], edge_recv.at[1 - side, k], (sim, step)))
+        for i, (first, to, sim) in enumerate(((0, EDGE + rows, below), (rows - 8, 0, above))):
+            plan.append((density.at[:, pl.ds(first, 8), :], ext.at[0, :, pl.ds(to, 8), :], row_send.at[i, 0], row_recv.at[i, 0], (sim, t)))
+            plan.append((momentum.at[:, :, pl.ds(first, 8), :], ext.at[pl.ds(1, 3), :, pl.ds(to, 8), :], row_send.at[i, 1], row_recv.at[i, 1], (sim, t)))
+            plan.append((energy.at[:, pl.ds(first, 8), :], ext.at[4, :, pl.ds(to, 8), :], row_send.at[i, 2], row_recv.at[i, 2], (sim, t)))
+        return [
+            pltpu.make_async_remote_copy(
+                src_ref=a, dst_ref=b, send_sem=c, recv_sem=d, device_id=e, device_id_type=MESH
+            )
+            for a, b, c, d, e in plan
+        ]
 
     c = cosines()
     a1, b1 = float(c[1, 0]), float(c[1, 1])
 
-    def transform(f, carry):
+    def transformed(f, with_edges):
         parts = []
         for plane in range(PLANES):
-            added = []
-            for r in range(tiles + 2):
-                k = 0 if r == 0 else 2 if r == tiles + 1 else 1
-                at = 4 * ((r - 1) % tiles) + plane
-                low = pltpu.roll(edge_term[0, k, f], at + 1, 1)
-                high = edge_term[1, k, f] if at == 127 else pltpu.roll(edge_term[1, k, f], 127 - at, 1)
-                added.append(jnp.where(lane == 0, low, jnp.where(lane == LANES - 1, high, 0.0)))
-            height = rows + 2 * EDGE
-            updated = center[f, plane] + jnp.concatenate(added, axis=0)
+            updated = center[f, plane]
+            if with_edges:
+                added = []
+                for r in range(tiles + 2):
+                    k = 0 if r == 0 else 2 if r == tiles + 1 else 1
+                    at = 4 * ((r - 1) % tiles) + plane
+                    low = pltpu.roll(edge_term[0, k, f], at + 1, 1)
+                    high = edge_term[1, k, f] if at == 127 else pltpu.roll(edge_term[1, k, f], 127 - at, 1)
+                    added.append(jnp.where(lane == 0, low, jnp.where(lane == LANES - 1, high, 0.0)))
+                updated += jnp.concatenate(added, axis=0)
             updated += pltpu.roll(from_above[f, plane], height - 1, 0)
             updated += pltpu.roll(from_below[f, plane], 1, 0)
-            parts.append(jnp.dot(rows_ref[...], updated, precision=HIGH, preferred_element_type=jnp.float32))
+            parts.append(product(rows_ref[...], updated))
         outer_sum, inner_sum = parts[0] + parts[3], parts[1] + parts[2]
         outer_gap, inner_gap = parts[0] - parts[3], parts[1] - parts[2]
         mixed = jnp.concatenate(
@@ -277,28 +289,93 @@
             ],
             axis=0,
         )
-        done = jnp.dot(mixed, brick_ref[...], precision=HIGH, preferred_element_type=jnp.float32)
+        done = product(mixed, brick_ref[...])
+        return [done[k * rows : (k + 1) * rows] for k in range(PLANES)]
+
+    last = n_section - 1
+    is_inside = jnp.logical_and(t > 0, t < last)
+
+    def early(f, carry):
+        for k, plane in enumerate(transformed(f, False)):
+            outbox[:, f, k] = plane.reshape(n_section, 4, LANES)
+
+        @pl.when(f == 0)
+        def _():
+            pl.semaphore_wait(barrier, greetings)
+            for copy in halo_copies():
+                copy.start()
+
+            def send_small(d, carry):
+                to = (t + d) % n_section
+                send(members, member_rows.at[t], member_send, member_recv, (s, to))
+                send(fringe_out.at[to], fringe.at[t], fringe_send, fringe_recv, (s, to))
+                return carry
+
+            lax.fori_loop(1, n_section, send_small, 0)
+            pltpu.make_async_copy(fringe_out.at[t], fringe.at[t], fringe_own).start()
+
+        def deliver(d, carry):
+            to = 1 + (t + d) % (n_section - 2)
+
+            @pl.when(to != t)
+            def _():
+                send(outbox.at[to, f], landed.at[t, f], bulk_send, bulk_recv, (s, to))
+
+            return carry
+
+        lax.fori_loop(0, n_section - 2, deliver, 0)
+
+        @pl.when(is_inside)
+        def _():
+            pltpu.make_async_copy(outbox.at[t, f], landed.at[t, f], own_sem).start()
+
+        return carry
+
+    lax.fori_loop(0, FIELDS, early, 0)
+
+    for copy in halo_copies():
+        copy.wait_recv()
+
+    def edges(k, carry):
+        for side in range(2):
+            terms = state_terms([edge_in[side, k, f] for f in range(FIELDS)])[1 - side]
+            for f in range(FIELDS):
+                edge_term[side, k, f] = terms[f]
+        return carry
+
+    lax.fori_loop(0, 3, edges, 0)
+
+    def outer(plane, carry):
+        cells(plane, 0)
+        cells(plane, tiles + 1)
+        return carry
+
+    lax.fori_loop(0, PLANES, outer, 0)
+
+    def complete(f, carry):
         peak = None
-        for k in range(PLANES):
-            plane = done[k * rows : (k + 1) * rows]
-            outbox[:, f, k] = plane.reshape(n_section, 4, LANES)
+        for k, plane in enumerate(transformed(f, True)):
+            late[0, f, k] = plane[0:4]
+            late[1, f, k] = plane[rows - 4 : rows]
             peak = jnp.abs(plane) if peak is None else jnp.maximum(peak, jnp.abs(plane))
         peak = jnp.maximum(peak, pltpu.roll(peak, 32, 1))
         peak = jnp.maximum(peak, pltpu.roll(peak, 64, 1))
         peak = jnp.maximum(peak, pltpu.roll(peak, rows - 1, 0))
         peak = jnp.maximum(peak, pltpu.roll(peak, rows - 2, 0))
         folded[f, pl.ds(0, rows), :] = peak
-
-        def deliver(d, carry):
-            to = (t + d) % n_section
-            send(outbox.at[to, f], landed.at[t, f], bulk_send, bulk_recv, (s, to))
-            return carry
-
-        lax.fori_loop(1, n_section, deliver, 0)
-        pltpu.make_async_copy(outbox.at[t, f], landed.at[t, f], own_sem).start()
+        for i, to in ((0, 0), (1, last)):
+
+            @pl.when(t != to)
+            def _():
+                send(late.at[i, f], landed.at[t, f], bulk_send, bulk_recv, (s, to))
+
+            @pl.when(t == to)
+            def _():
+                pltpu.make_async_copy(late.at[i, f], landed.at[t, f], own_sem).start()
+
         return carry
 
-    lax.fori_loop(0, FIELDS, transform, 0)
+    lax.fori_loop(0, FIELDS, complete, 0)
 
     some = pl.ds(0, n_section - 1)
     arrived(member_rows.at[some], member_recv)
@@ -371,8 +448,11 @@
     for i in range(shards):
         final[pl.ds(i * depth, depth), :] = full[i]
 
-    for copy in sends:
+    for copy in halo_copies():
         copy.wait_send()
+    arrived(fringe.at[some], fringe_recv)
+    arrived(fringe_out.at[some], fringe_send)
+    arrived(fringe_out.at[0], fringe_own)
     arrived(member_rows.at[some], member_send)
     arrived(outbox.at[some], bulk_send)
     arrived(pass1, red_send.at[0])
@@ -384,7 +464,7 @@
     arrived(landed.at[some], bulk_recv)
 
 
-def place_kernel(slot_ref, final, members, landed, coded, group_peak, peaks, scale):
+def place_kernel(slot_ref, final, members, landed, fringe, coded, group_peak, peaks, scale, beside, added):
     n_section = landed.shape[0]
     columns = GROUPS // LANES
 
@@ -413,13 +493,28 @@
                     full = jnp.where(lane // 32 == a, turned[(a - q) % 4], full)
                 for f in range(FIELDS):
                     scale[f, 4 * block + q] = full[f : f + 1]
+        edges = fringe[...].reshape(4 * n_section, LANES)
+        side = lax.broadcasted_iota(jnp.int32, edges.shape, 1)
+        beside[...] = jnp.where(side < 64, pltpu.roll(edges, 4 * n_section - 4, 0), pltpu.roll(edges, 4, 0))
 
     f = pl.program_id(0)
+    c = cosines()
+    edges = beside[...]
+    side = lax.broadcasted_iota(jnp.int32, edges.shape, 1)
+    first = jnp.zeros(edges.shape, jnp.float32)
+    final_cell = jnp.zeros(edges.shape, jnp.float32)
+    for k in range(4):
+        first = jnp.where(side == 32 * k, float(c[k, 0]), first)
+        final_cell = jnp.where(side == 32 * k + 31, float(c[k, 3]), final_cell)
+    for k in range(PLANES):
+        extra = final_cell * edges[:, k : k + 1] + first * edges[:, 64 + k : 65 + k]
+        added[:, k] = extra.reshape(n_section, 4, LANES)
+    beside[...] = pltpu.roll(edges, LANES - PLANES, 1)
 
     for b in range(n_section):
         slot = slot_ref[0, b]
         divisor = scale[f, slot]
-        coded[0, :, :, pl.ds(pl.multiple_of(slot * LANES, LANES), LANES)] = landed[b, 0] / divisor[None]
+        coded[0, :, :, pl.ds(pl.multiple_of(slot * LANES, LANES), LANES)] = (landed[b, 0] + added[b]) / divisor[None]
 
 
 def per_device(density, momentum, energy, membership, slot_of_brick):
@@ -433,20 +528,24 @@
     vmem, anywhere = pl.BlockSpec(memory_space=pltpu.VMEM), pl.BlockSpec(memory_space=pl.ANY)
     smem = pl.BlockSpec(memory_space=pltpu.SMEM)
     dma = pltpu.SemaphoreType.DMA
-    landed, final = pl.pallas_call(
+    landed, fringe, final = pl.pallas_call(
         step_kernel,
         out_shape=(
             jax.ShapeDtypeStruct((n_section, FIELDS, planes, 4, width), f32),
+            jax.ShapeDtypeStruct((n_section, 4, width), f32),
             jax.ShapeDtypeStruct((64, width), f32),
         ),
-        in_specs=[vmem, anywhere, anywhere, anywhere, anywhere, vmem, vmem],
-        out_specs=(anywhere, vmem),
+        in_specs=[vmem, anywhere, anywhere, anywhere, anywhere, vmem, vmem, vmem],
+        out_specs=(anywhere, anywhere, vmem),
         scratch_shapes=[
             pltpu.VMEM((FIELDS, planes, height, width), f32),
             pltpu.VMEM((FIELDS, planes, height, width), f32),
             pltpu.VMEM((FIELDS, planes, height, width), f32),
             pltpu.VMEM((FIELDS, planes, height, width), f32),
             pltpu.VMEM((n_section, FIELDS, planes, 4, width), f32),
+            pltpu.VMEM((2, FIELDS, planes, 4, width), f32),
+            pltpu.VMEM((height, width), f32),
+            pltpu.VMEM((n_section, 4, width), f32),
             pltpu.VMEM((FIELDS, 4 * block_rows, width), f32),
             pltpu.VMEM((n_section, 1, membership.shape[1]), jnp.int32),
             pltpu.VMEM((n_section // 4, block_rows, width), jnp.int32),
@@ -470,12 +569,15 @@
             dma,
             dma,
             dma,
+            dma,
+            dma,
+            dma,
             dma((4,)),
             dma((4,)),
         ],
         compiler_params=pltpu.CompilerParams(collective_id=0, has_side_effects=True),
         name="step",
-    )(slot_of_brick, density, momentum, energy, membership, row_matrix(rows), brick_matrix())
+    )(slot_of_brick, density, momentum, energy, membership, row_matrix(rows), brick_matrix(), depth_matrix())
     return pl.pallas_call(
         place_kernel,
         grid=(FIELDS,),
@@ -488,14 +590,20 @@
             pl.BlockSpec((64, width), lambda f: (0, 0)),
             pl.BlockSpec(membership.shape, lambda f: (0, 0)),
             pl.BlockSpec((n_section, 1, planes, 4, width), lambda f: (0, f, 0, 0, 0)),
+            pl.BlockSpec((n_section, 4, width), lambda f: (0, 0, 0)),
         ],
         out_specs=(
             pl.BlockSpec((1, planes, 4, n_section * width), lambda f: (f, 0, 0, 0)),
             pl.BlockSpec((FIELDS, GROUPS), lambda f: (0, 0)),
         ),
-        scratch_shapes=[pltpu.VMEM((8, GROUPS), f32), pltpu.VMEM((FIELDS, n_section, 1, width), f32)],
+        scratch_shapes=[
+            pltpu.VMEM((8, GROUPS), f32),
+            pltpu.VMEM((FIELDS, n_section, 1, width), f32),
+            pltpu.VMEM((rows, width), f32),
+            pltpu.VMEM((n_section, planes, 4, width), f32),
+        ],
         name="place",
-    )(slot_of_brick, final, membership, landed)
+    )(slot_of_brick, final, membership, landed, fringe)
 
 
 def solution(mesh):

time: 75.1 us -> 75.8 us (level)
  no operation moved by 1% of the time
where the time goes in v2:
time: 75.8 us; the launch traced here: 75.5 us
  Pallas kernels  74.8 us (99%)
    pallas_call x1, Pallas kernels, per_device(): pl.pallas_call(step_kernel, out_shape=(jax.ShapeDtypeStruct((n_section, F...  70.1 us
    pallas_call x1, Pallas kernels, per_device(): pl.pallas_call(place_kernel, grid=(FIELDS,), out_shape=(jax.ShapeDtypeStr...  4.71 us

profile of v2, /device:TPU:1, one launch (start us, length us, event | category | flops | bytes accessed | tf_op | source)
XLA Modules:
  0.0 75.5 jit_solution(10268744846542564367)
XLA Ops:
  0.6 70.1 %step.1 = (f32[24,5,4,4,128]{4,3,2,1,0:T(4,128)}, f32[24,4,128]{2,1,0:T(4,128)}, f32[64,128]{1,0:T(8,128)}) custom-call(s32[1,24]{1,0:T(1,128)} %slot_ref.3, f32[4,96,128]{2,1,0:T(8,128)} %density.1, f32[3,4,96,128]{3,2,1,0:T(8,128)} %momentum.1, f32[4,96,128]{2,1,0:T(8,128)} %energy.1, s32[1,768]{1,0:T(1,128)} %members.3, ...), custom_call_target="tpu_custom_call" | custom-call | tf_op jit(solution)/shard_map/step/pallas_call | solution.py:531
  70.8 4.7 %place.1 = (f32[5,4,4,3072]{3,2,1,0:T(4,128)}, f32[5,1536]{1,0:T(8,128)}) custom-call(s32[1,24]{1,0:T(1,128)} %slot_ref.3, f32[64,128]{1,0:T(8,128)} %get-tuple-element.5.final, s32[1,768]{1,0:T(1,128)} %members.3, f32[24,5,4,4,128]{4,3,2,1,0:T(4,128)} %get-tuple-element.6.landed, f32[24,4,128]{2,1,0:T(4,128)} %get-tuple-element.7.fringe), custom_call_target="tpu_custom_call" | custom-call | tf_op jit(solution)/shard_map/place/pallas_call | solution.py:581

commit v3 on v2

--- a/solution.py
+++ b/solution.py
@@ -13,6 +13,7 @@
 GAMMA_LESS, COURANT, DIFFUSE, EPSILON = 0.4, 0.05, 0.1, 1e-06
 FIELDS, PLANES, LANES, EDGE = 5, 4, 128, 8
 GROUPS = 1536
+AT_ONCE = 3
 HIGH = lax.Precision.HIGHEST
 MESH = pl.DeviceIdType.MESH
 
@@ -295,6 +296,22 @@
     last = n_section - 1
     is_inside = jnp.logical_and(t > 0, t < last)
 
+    def deliver(f):
+        def visit(d, carry):
+            to = 1 + (t + d) % (n_section - 2)
+
+            @pl.when(to != t)
+            def _():
+                send(outbox.at[to, f], landed.at[t, f], bulk_send, bulk_recv, (s, to))
+
+            return carry
+
+        lax.fori_loop(0, n_section - 2, visit, 0)
+
+        @pl.when(is_inside)
+        def _():
+            pltpu.make_async_copy(outbox.at[t, f], landed.at[t, f], own_sem).start()
+
     def early(f, carry):
         for k, plane in enumerate(transformed(f, False)):
             outbox[:, f, k] = plane.reshape(n_section, 4, LANES)
@@ -314,20 +331,9 @@
             lax.fori_loop(1, n_section, send_small, 0)
             pltpu.make_async_copy(fringe_out.at[t], fringe.at[t], fringe_own).start()
 
-        def deliver(d, carry):
-            to = 1 + (t + d) % (n_section - 2)
-
-            @pl.when(to != t)
-            def _():
-                send(outbox.at[to, f], landed.at[t, f], bulk_send, bulk_recv, (s, to))
-
-            return carry
-
-        lax.fori_loop(0, n_section - 2, deliver, 0)
-
-        @pl.when(is_inside)
+        @pl.when(f < AT_ONCE)
         def _():
-            pltpu.make_async_copy(outbox.at[t, f], landed.at[t, f], own_sem).start()
+            deliver(f)
 
         return carry
 
@@ -423,6 +429,7 @@
     for d in range(1, shards):
         other = (place + d) % shards
         send(own.at[other], pass1.at[d - 1], red_send.at[0], red_recv.at[0], in_plane(d))
+    deliver(AT_ONCE)
     arrived(pass1, red_recv.at[0])
     value = own[place]
     for d in range(shards - 1):
@@ -437,6 +444,8 @@
     hold[1] = value
     for d in range(1, z_all):
         send(hold.at[1], pass3.at[d - 1], red_send.at[2], red_recv.at[2], in_depth(d))
+    for f in range(AT_ONCE + 1, FIELDS):
+        deliver(f)
     arrived(pass3, red_recv.at[2])
     for d in range(z_all - 1):
         value = jnp.maximum(value, pass3[d])
@@ -485,7 +494,7 @@
                     peaks[:, col * LANES : (col + 1) * LANES], low, axis=1, mode="promise_in_bounds"
                 )
                 found = jnp.where(high == col, picked, found)
-            found = found + EPSILON
+            found = 1.0 / (found + EPSILON)
             turned = [found] + [pltpu.roll(found, 32 * q, 1) for q in range(1, 4)]
             for q in range(4):
                 full = turned[(0 - q) % 4]
@@ -513,8 +522,8 @@
 
     for b in range(n_section):
         slot = slot_ref[0, b]
-        divisor = scale[f, slot]
-        coded[0, :, :, pl.ds(pl.multiple_of(slot * LANES, LANES), LANES)] = (landed[b, 0] + added[b]) / divisor[None]
+        factor = scale[f, slot]
+        coded[0, :, :, pl.ds(pl.multiple_of(slot * LANES, LANES), LANES)] = (landed[b, 0] + added[b]) * factor[None]
 
 
 def per_device(density, momentum, energy, membership, slot_of_brick):

time: 75.8 us -> 74.8 us (0.987)
  Pallas kernels: 74.8 us -> 73.9 us
    pallas_call x1, Pallas kernels: 70.1 us -> 69.2 us  [per_device(): pl.pallas_call(step_kernel, out_shape=(jax.ShapeDtypeStruct((n_section, F...]
where the time goes in v3:
time: 74.8 us; the launch traced here: 74.5 us
  Pallas kernels  73.9 us (99%)
    pallas_call x1, Pallas kernels, per_device(): pl.pallas_call(step_kernel, out_shape=(jax.ShapeDtypeStruct((n_section, F...  69.2 us
    pallas_call x1, Pallas kernels, per_device(): pl.pallas_call(place_kernel, grid=(FIELDS,), out_shape=(jax.ShapeDtypeStr...  4.73 us

profile of v3, /device:TPU:1, one launch (start us, length us, event | category | flops | bytes accessed | tf_op | source)
XLA Modules:
  0.0 74.5 jit_solution(441222874436752374)
XLA Ops:
  0.6 69.2 %step.1 = (f32[24,5,4,4,128]{4,3,2,1,0:T(4,128)}, f32[24,4,128]{2,1,0:T(4,128)}, f32[64,128]{1,0:T(8,128)}) custom-call(s32[1,24]{1,0:T(1,128)} %slot_ref.3, f32[4,96,128]{2,1,0:T(8,128)} %density.1, f32[3,4,96,128]{3,2,1,0:T(8,128)} %momentum.1, f32[4,96,128]{2,1,0:T(8,128)} %energy.1, s32[1,768]{1,0:T(1,128)} %members.3, ...), custom_call_target="tpu_custom_call" | custom-call | tf_op jit(solution)/shard_map/step/pallas_call | solution.py:540
  69.8 4.7 %place.1 = (f32[5,4,4,3072]{3,2,1,0:T(4,128)}, f32[5,1536]{1,0:T(8,128)}) custom-call(s32[1,24]{1,0:T(1,128)} %slot_ref.3, f32[64,128]{1,0:T(8,128)} %get-tuple-element.5.final, s32[1,768]{1,0:T(1,128)} %members.3, f32[24,5,4,4,128]{4,3,2,1,0:T(4,128)} %get-tuple-element.6.landed, f32[24,4,128]{2,1,0:T(4,128)} %get-tuple-element.7.fringe), custom_call_target="tpu_custom_call" | custom-call | tf_op jit(solution)/shard_map/place/pallas_call | solution.py:590

commit v4 on v3

--- a/solution.py
+++ b/solution.py
@@ -13,7 +13,6 @@
 GAMMA_LESS, COURANT, DIFFUSE, EPSILON = 0.4, 0.05, 0.1, 1e-06
 FIELDS, PLANES, LANES, EDGE = 5, 4, 128, 8
 GROUPS = 1536
-AT_ONCE = 3
 HIGH = lax.Precision.HIGHEST
 MESH = pl.DeviceIdType.MESH
 
@@ -32,6 +31,14 @@
         predict[y, [at - 1, at + 1]] = -9.0 / 16.0
         predict[y, [at - 3, at + 3]] = 1.0 / 16.0
     return (np.kron(np.eye(rows // 4), cosines()) @ predict).astype(np.float32)
+
+
+def outer_matrix(rows):
+    whole = row_matrix(rows)
+    out = np.zeros((8, 32), np.float32)
+    out[:4, :16] = whole[:4, :16]
+    out[4:, 16:] = whole[rows - 4 :, rows:]
+    return out
 
 
 def brick_matrix():
@@ -74,6 +81,7 @@
     rows_ref,
     brick_ref,
     depth_ref,
+    outer_ref,
     landed,
     fringe,
     final,
@@ -84,6 +92,9 @@
     outbox,
     late,
     edge_rows,
+    planes_done,
+    beside,
+    beyond_mixed,
     fringe_out,
     folded,
     member_rows,
@@ -186,7 +197,7 @@
                 value = ext[f, plane, pl.ds(EDGE + 8 * r, 8), :]
                 at = 4 * r + plane
                 low = jnp.where(lane == at, pltpu.roll(value, at, 1) if at else value, low)
-                high = jnp.where(lane == 127 - at, pltpu.roll(value, 128 - at, 1) if at else value, high)
+                high = jnp.where(lane == at, pltpu.roll(value, at + 1, 1), high)
         edge_out[0, f] = low
         edge_out[1, f] = high
         return carry
@@ -263,25 +274,10 @@
     c = cosines()
     a1, b1 = float(c[1, 0]), float(c[1, 1])
 
-    def transformed(f, with_edges):
-        parts = []
-        for plane in range(PLANES):
-            updated = center[f, plane]
-            if with_edges:
-                added = []
-                for r in range(tiles + 2):
-                    k = 0 if r == 0 else 2 if r == tiles + 1 else 1
-                    at = 4 * ((r - 1) % tiles) + plane
-                    low = pltpu.roll(edge_term[0, k, f], at + 1, 1)
-                    high = edge_term[1, k, f] if at == 127 else pltpu.roll(edge_term[1, k, f], 127 - at, 1)
-                    added.append(jnp.where(lane == 0, low, jnp.where(lane == LANES - 1, high, 0.0)))
-                updated += jnp.concatenate(added, axis=0)
-            updated += pltpu.roll(from_above[f, plane], height - 1, 0)
-            updated += pltpu.roll(from_below[f, plane], 1, 0)
-            parts.append(product(rows_ref[...], updated))
+    def mix(parts):
         outer_sum, inner_sum = parts[0] + parts[3], parts[1] + parts[2]
         outer_gap, inner_gap = parts[0] - parts[3], parts[1] - parts[2]
-        mixed = jnp.concatenate(
+        return jnp.concatenate(
             [
                 0.5 * (outer_sum + inner_sum),
                 a1 * outer_gap + b1 * inner_gap,
@@ -290,19 +286,28 @@
             ],
             axis=0,
         )
-        done = product(mixed, brick_ref[...])
+
+    def transformed(f):
+        parts = []
+        for plane in range(PLANES):
+            updated = center[f, plane] + pltpu.roll(from_above[f, plane], height - 1, 0)
+            updated += pltpu.roll(from_below[f, plane], 1, 0)
+            parts.append(product(rows_ref[...], updated))
+        done = product(mix(parts), brick_ref[...])
         return [done[k * rows : (k + 1) * rows] for k in range(PLANES)]
 
     last = n_section - 1
     is_inside = jnp.logical_and(t > 0, t < last)
 
-    def deliver(f):
+    def deliver(first, count):
+        some_fields = pl.ds(first, count)
+
         def visit(d, carry):
             to = 1 + (t + d) % (n_section - 2)
 
             @pl.when(to != t)
             def _():
-                send(outbox.at[to, f], landed.at[t, f], bulk_send, bulk_recv, (s, to))
+                send(outbox.at[to, some_fields], landed.at[t, some_fields], bulk_send, bulk_recv, (s, to))
 
             return carry
 
@@ -310,11 +315,12 @@
 
         @pl.when(is_inside)
         def _():
-            pltpu.make_async_copy(outbox.at[t, f], landed.at[t, f], own_sem).start()
+            pltpu.make_async_copy(outbox.at[t, some_fields], landed.at[t, some_fields], own_sem).start()
 
     def early(f, carry):
-        for k, plane in enumerate(transformed(f, False)):
+        for k, plane in enumerate(transformed(f)):
             outbox[:, f, k] = plane.reshape(n_section, 4, LANES)
+            planes_done[f, k] = plane
 
         @pl.when(f == 0)
         def _():
@@ -331,9 +337,9 @@
             lax.fori_loop(1, n_section, send_small, 0)
             pltpu.make_async_copy(fringe_out.at[t], fringe.at[t], fringe_own).start()
 
-        @pl.when(f < AT_ONCE)
+        @pl.when(f == 2)
         def _():
-            deliver(f)
+            deliver(0, 3)
 
         return carry
 
@@ -358,30 +364,74 @@
 
     lax.fori_loop(0, PLANES, outer, 0)
 
+    group = lane // PLANES
+    for r in range(tiles + 2):
+        k = 0 if r == 0 else 2 if r == tiles + 1 else 1
+        at = (r - 1) % tiles
+        packed = nothing
+        for f in range(FIELDS):
+            packed = jnp.where(group == f, pltpu.roll(edge_term[1, k, f], (4 * (f - at)) % LANES, 1), packed)
+            packed = jnp.where(group == 16 + f, pltpu.roll(edge_term[0, k, f], (64 + 4 * (f - at)) % LANES, 1), packed)
+        edge_rows[pl.ds(8 * r, 8), :] = packed
+    beside[...] = product(product(rows_ref[...], edge_rows[...]), depth_ref[...])
+
+    def beyond(f, carry):
+        parts = []
+        for plane in range(PLANES):
+            halves = []
+            for first, low in ((0, True), (height - 8, False)):
+                tile = [ref[f, plane, pl.ds(first, 8), :] for ref in (center, from_above, from_below)]
+                both = [jnp.concatenate([a, nothing] if low else [nothing, a], axis=0) for a in tile]
+                halves.append(both[0] + pltpu.roll(both[1], 15, 0) + pltpu.roll(both[2], 1, 0))
+            parts.append(jnp.concatenate(halves, axis=0))
+        made = product(outer_ref[...], jnp.concatenate(parts, axis=1))
+        beyond_mixed[pl.ds(pl.multiple_of(32 * f, 32), 32), :] = mix(
+            [made[:, LANES * k : LANES * (k + 1)] for k in range(PLANES)]
+        )
+        return carry
+
+    lax.fori_loop(0, FIELDS, beyond, 0)
+    beyond_mixed[...] = product(beyond_mixed[...], brick_ref[...])
+
+    wide_lane = lax.broadcasted_iota(jnp.int32, (rows, LANES), 1)
+    first_cell = jnp.zeros((rows, LANES), jnp.float32)
+    final_cell = jnp.zeros((rows, LANES), jnp.float32)
+    for k in range(4):
+        first_cell = jnp.where(wide_lane == 32 * k, float(c[k, 0]), first_cell)
+        final_cell = jnp.where(wide_lane == 32 * k + 31, float(c[k, 3]), final_cell)
+    upper = lax.broadcasted_iota(jnp.int32, (8, LANES), 0) < 4
+
     def complete(f, carry):
         peak = None
-        for k, plane in enumerate(transformed(f, True)):
-            late[0, f, k] = plane[0:4]
-            late[1, f, k] = plane[rows - 4 : rows]
-            peak = jnp.abs(plane) if peak is None else jnp.maximum(peak, jnp.abs(plane))
+        columns_now = beside[...]
+        for k in range(PLANES):
+            plane = planes_done[f, k] + final_cell * columns_now[:, k : k + 1] + first_cell * columns_now[:, 64 + k : 65 + k]
+            outside = beyond_mixed[pl.ds(pl.multiple_of(32 * f + 8 * k, 8), 8), :]
+            top = plane[0:8] + jnp.where(upper, outside, 0.0)
+            bottom = plane[rows - 8 : rows] + jnp.where(upper, 0.0, outside)
+            late[0, f, k] = top[0:4]
+            late[1, f, k] = bottom[4:8]
+            plane = jnp.abs(jnp.concatenate([top, plane[8 : rows - 8], bottom], axis=0))
+            peak = plane if peak is None else jnp.maximum(peak, plane)
+        beside[...] = pltpu.roll(columns_now, LANES - PLANES, 1)
         peak = jnp.maximum(peak, pltpu.roll(peak, 32, 1))
         peak = jnp.maximum(peak, pltpu.roll(peak, 64, 1))
         peak = jnp.maximum(peak, pltpu.roll(peak, rows - 1, 0))
         peak = jnp.maximum(peak, pltpu.roll(peak, rows - 2, 0))
         folded[f, pl.ds(0, rows), :] = peak
-        for i, to in ((0, 0), (1, last)):
-
-            @pl.when(t != to)
-            def _():
-                send(late.at[i, f], landed.at[t, f], bulk_send, bulk_recv, (s, to))
-
-            @pl.when(t == to)
-            def _():
-                pltpu.make_async_copy(late.at[i, f], landed.at[t, f], own_sem).start()
-
         return carry
 
     lax.fori_loop(0, FIELDS, complete, 0)
+    for i, to in ((0, 0), (1, last)):
+
+        @pl.when(t != to)
+        def _():
+            send(late.at[i], landed.at[t], bulk_send, bulk_recv, (s, to))
+
+        @pl.when(t == to)
+        def _():
+            pltpu.make_async_copy(late.at[i], landed.at[t], own_sem).start()
+
 
     some = pl.ds(0, n_section - 1)
     arrived(member_rows.at[some], member_recv)
@@ -429,7 +479,6 @@
     for d in range(1, shards):
         other = (place + d) % shards
         send(own.at[other], pass1.at[d - 1], red_send.at[0], red_recv.at[0], in_plane(d))
-    deliver(AT_ONCE)
     arrived(pass1, red_recv.at[0])
     value = own[place]
     for d in range(shards - 1):
@@ -444,8 +493,7 @@
     hold[1] = value
     for d in range(1, z_all):
         send(hold.at[1], pass3.at[d - 1], red_send.at[2], red_recv.at[2], in_depth(d))
-    for f in range(AT_ONCE + 1, FIELDS):
-        deliver(f)
+    deliver(3, 2)
     arrived(pass3, red_recv.at[2])
     for d in range(z_all - 1):
         value = jnp.maximum(value, pass3[d])
@@ -544,7 +592,7 @@
             jax.ShapeDtypeStruct((n_section, 4, width), f32),
             jax.ShapeDtypeStruct((64, width), f32),
         ),
-        in_specs=[vmem, anywhere, anywhere, anywhere, anywhere, vmem, vmem, vmem],
+        in_specs=[vmem, anywhere, anywhere, anywhere, anywhere, vmem, vmem, vmem, vmem],
         out_specs=(anywhere, anywhere, vmem),
         scratch_shapes=[
             pltpu.VMEM((FIELDS, planes, height, width), f32),
@@ -554,6 +602,9 @@
             pltpu.VMEM((n_section, FIELDS, planes, 4, width), f32),
             pltpu.VMEM((2, FIELDS, planes, 4, width), f32),
             pltpu.VMEM((height, width), f32),
+            pltpu.VMEM((FIELDS, planes, rows, width), f32),
+            pltpu.VMEM((rows, width), f32),
+            pltpu.VMEM((FIELDS * 32, width), f32),
             pltpu.VMEM((n_section, 4, width), f32),
             pltpu.VMEM((FIELDS, 4 * block_rows, width), f32),
             pltpu.VMEM((n_section, 1, membership.shape[1]), jnp.int32),
@@ -586,7 +637,7 @@
         ],
         compiler_params=pltpu.CompilerParams(collective_id=0, has_side_effects=True),
         name="step",
-    )(slot_of_brick, density, momentum, energy, membership, row_matrix(rows), brick_matrix(), depth_matrix())
+    )(slot_of_brick, density, momentum, energy, membership, row_matrix(rows), brick_matrix(), depth_matrix(), outer_matrix(rows))
     return pl.pallas_call(
         place_kernel,
         grid=(FIELDS,),

time: 74.8 us -> 72.4 us (0.968)
  the two profiles are of different devices: /device:TPU:1 before, /device:TPU:14 now
where the time goes in v4:
time: 72.4 us; the launch traced here: 72.2 us
  Pallas kernels  71.5 us (99%)
    pallas_call x1, Pallas kernels, per_device(): pl.pallas_call(step_kernel, out_shape=(jax.ShapeDtypeStruct((n_section, F...  66.8 us
    pallas_call x1, Pallas kernels, per_device(): pl.pallas_call(place_kernel, grid=(FIELDS,), out_shape=(jax.ShapeDtypeStr...  4.73 us

profile of v4, /device:TPU:14, one launch (start us, length us, event | category | flops | bytes accessed | tf_op | source)
XLA Modules:
  0.0 72.2 jit_solution(7958889382458341409)
XLA Ops:
  0.6 66.8 %step.1 = (f32[24,5,4,4,128]{4,3,2,1,0:T(4,128)}, f32[24,4,128]{2,1,0:T(4,128)}, f32[64,128]{1,0:T(8,128)}) custom-call(s32[1,24]{1,0:T(1,128)} %slot_ref.3, f32[4,96,128]{2,1,0:T(8,128)} %density.1, f32[3,4,96,128]{3,2,1,0:T(8,128)} %momentum.1, f32[4,96,128]{2,1,0:T(8,128)} %energy.1, s32[1,768]{1,0:T(1,128)} %members.3, ...), custom_call_target="tpu_custom_call" | custom-call | tf_op jit(solution)/shard_map/step/pallas_call | solution.py:588
  67.4 4.7 %place.1 = (f32[5,4,4,3072]{3,2,1,0:T(4,128)}, f32[5,1536]{1,0:T(8,128)}) custom-call(s32[1,24]{1,0:T(1,128)} %slot_ref.3, f32[64,128]{1,0:T(8,128)} %get-tuple-element.5.final, s32[1,768]{1,0:T(1,128)} %members.3, f32[24,5,4,4,128]{4,3,2,1,0:T(4,128)} %get-tuple-element.6.landed, f32[24,4,128]{2,1,0:T(4,128)} %get-tuple-element.7.fringe), custom_call_target="tpu_custom_call" | custom-call | tf_op jit(solution)/shard_map/place/pallas_call | solution.py:641

commit v5 on v4

--- a/solution.py
+++ b/solution.py
@@ -150,17 +150,17 @@
         copy.start()
 
     barrier = pltpu.get_barrier_semaphore()
-    shards = CORES * X_CHIPS
-    place = core * X_CHIPS + x
+    shards = CORES * Y_CHIPS
+    place = core * Y_CHIPS + y
     z_all = Z_HI * Z_LO
     z = z_hi * Z_LO + z_lo
 
     def in_plane(step):
         other = (place + step) % shards
-        return (s - core + other // X_CHIPS, (other % X_CHIPS) * Z_LO + z_lo)
+        return (z_hi * (CORES * Y_CHIPS) + (other % Y_CHIPS) * CORES + other // Y_CHIPS, t)
 
     def in_column(step):
-        return (s + ((y + step) % Y_CHIPS - y) * CORES, t)
+        return (s, ((x + step) % X_CHIPS) * Z_LO + z_lo)
 
     def in_depth(step):
         other = (z + step) % z_all
@@ -177,14 +177,12 @@
     for sim in (below, above):
         for section in (left, t, right):
             greet((sim, section))
-    for d in range(1, X_CHIPS):
-        greet((s + 1 - 2 * core, ((x + d) % X_CHIPS) * Z_LO + z_lo))
-    for d in range(1, Y_CHIPS):
-        greet(in_column(d))
+    for d in range(1, shards):
+        greet(in_plane(d))
     if Z_HI > 1:
         for d in range(Z_LO):
             greet(((s + n_sim // 2) % n_sim, x * Z_LO + d))
-    greetings = (n_section - 1) + 6 + (X_CHIPS - 1) + (Y_CHIPS - 1) + (Z_LO if Z_HI > 1 else 0)
+    greetings = (n_section - 1) + 6 + (shards - 1) + (Z_LO if Z_HI > 1 else 0)
 
     for copy in loads:
         copy.wait()
@@ -483,12 +481,12 @@
     value = own[place]
     for d in range(shards - 1):
         value = jnp.maximum(value, pass1[d])
-    if Y_CHIPS > 1:
+    if X_CHIPS > 1:
         hold[0] = value
-        for d in range(1, Y_CHIPS):
+        for d in range(1, X_CHIPS):
             send(hold.at[0], pass2.at[d - 1], red_send.at[1], red_recv.at[1], in_column(d))
         arrived(pass2, red_recv.at[1])
-        for d in range(Y_CHIPS - 1):
+        for d in range(X_CHIPS - 1):
             value = jnp.maximum(value, pass2[d])
     hold[1] = value
     for d in range(1, z_all):
@@ -513,7 +511,7 @@
     arrived(member_rows.at[some], member_send)
     arrived(outbox.at[some], bulk_send)
     arrived(pass1, red_send.at[0])
-    if Y_CHIPS > 1:
+    if X_CHIPS > 1:
         arrived(pass2, red_send.at[1])
     arrived(pass3, red_send.at[2])
     arrived(pass1, red_send.at[3])
@@ -521,64 +519,64 @@
     arrived(landed.at[some], bulk_recv)
 
 
-def place_kernel(slot_ref, final, members, landed, fringe, coded, group_peak, peaks, scale, beside, added):
+def place_kernel(slot_ref, final, members, landed, fringe, coded, group_peak, peaks, scale, added):
     n_section = landed.shape[0]
     columns = GROUPS // LANES
 
-    @pl.when(pl.program_id(0) == 0)
-    def _():
-        peaks[...] = jnp.zeros(peaks.shape, jnp.float32)
-        for f in range(FIELDS):
-            for col in range(columns):
-                peaks[f : f + 1, col * LANES : (col + 1) * LANES] = final[f * columns + col : f * columns + col + 1, :]
-        group_peak[...] = peaks[0:FIELDS, :]
-        lane = lax.broadcasted_iota(jnp.int32, (8, LANES), 1)
-        for block in range(n_section // 4):
-            label = jnp.broadcast_to(members[0:1, block * LANES : (block + 1) * LANES], (8, LANES))
-            high, low = label // LANES, label % LANES
-            found = jnp.zeros((8, LANES), jnp.float32)
-            for col in range(columns):
-                picked = jnp.take_along_axis(
-                    peaks[:, col * LANES : (col + 1) * LANES], low, axis=1, mode="promise_in_bounds"
-                )
-                found = jnp.where(high == col, picked, found)
-            found = 1.0 / (found + EPSILON)
-            turned = [found] + [pltpu.roll(found, 32 * q, 1) for q in range(1, 4)]
-            for q in range(4):
-                full = turned[(0 - q) % 4]
-                for a in range(1, 4):
-                    full = jnp.where(lane // 32 == a, turned[(a - q) % 4], full)
-                for f in range(FIELDS):
-                    scale[f, 4 * block + q] = full[f : f + 1]
-        edges = fringe[...].reshape(4 * n_section, LANES)
-        side = lax.broadcasted_iota(jnp.int32, edges.shape, 1)
-        beside[...] = jnp.where(side < 64, pltpu.roll(edges, 4 * n_section - 4, 0), pltpu.roll(edges, 4, 0))
-
-    f = pl.program_id(0)
+    peaks[...] = jnp.zeros(peaks.shape, jnp.float32)
+    for f in range(FIELDS):
+        for col in range(columns):
+            peaks[f : f + 1, col * LANES : (col + 1) * LANES] = final[f * columns + col : f * columns + col + 1, :]
+    group_peak[...] = peaks[0:FIELDS, :]
+    lane = lax.broadcasted_iota(jnp.int32, (8, LANES), 1)
+    for block in range(n_section // 4):
+        label = jnp.broadcast_to(members[0:1, block * LANES : (block + 1) * LANES], (8, LANES))
+        high, low = label // LANES, label % LANES
+        found = jnp.zeros((8, LANES), jnp.float32)
+        for col in range(columns):
+            picked = jnp.take_along_axis(
+                peaks[:, col * LANES : (col + 1) * LANES], low, axis=1, mode="promise_in_bounds"
+            )
+            found = jnp.where(high == col, picked, found)
+        found = 1.0 / (found + EPSILON)
+        turned = [found] + [pltpu.roll(found, 32 * q, 1) for q in range(1, 4)]
+        for q in range(4):
+            full = turned[(0 - q) % 4]
+            for a in range(1, 4):
+                full = jnp.where(lane // 32 == a, turned[(a - q) % 4], full)
+            for f in range(FIELDS):
+                scale[f, 4 * block + q] = full[f : f + 1]
+    edges = fringe[...].reshape(4 * n_section, LANES)
+    side = lax.broadcasted_iota(jnp.int32, edges.shape, 1)
+    edges = jnp.where(side < 64, pltpu.roll(edges, 4 * n_section - 4, 0), pltpu.roll(edges, 4, 0))
+
     c = cosines()
-    edges = beside[...]
-    side = lax.broadcasted_iota(jnp.int32, edges.shape, 1)
     first = jnp.zeros(edges.shape, jnp.float32)
     final_cell = jnp.zeros(edges.shape, jnp.float32)
     for k in range(4):
         first = jnp.where(side == 32 * k, float(c[k, 0]), first)
         final_cell = jnp.where(side == 32 * k + 31, float(c[k, 3]), final_cell)
-    for k in range(PLANES):
-        extra = final_cell * edges[:, k : k + 1] + first * edges[:, 64 + k : 65 + k]
-        added[:, k] = extra.reshape(n_section, 4, LANES)
-    beside[...] = pltpu.roll(edges, LANES - PLANES, 1)
-
-    for b in range(n_section):
+    for f in range(FIELDS):
+        for k in range(PLANES):
+            at = PLANES * f + k
+            extra = final_cell * edges[:, at : at + 1] + first * edges[:, 64 + at : 65 + at]
+            added[:, f, k] = extra.reshape(n_section, 4, LANES)
+
+    def visit(b, carry):
         slot = slot_ref[0, b]
-        factor = scale[f, slot]
-        coded[0, :, :, pl.ds(pl.multiple_of(slot * LANES, LANES), LANES)] = (landed[b, 0] + added[b]) * factor[None]
+        columns_now = pl.ds(pl.multiple_of(slot * LANES, LANES), LANES)
+        for f in range(FIELDS):
+            coded[f, :, :, columns_now] = (landed[b, f] + added[b, f]) * scale[f, slot][None]
+        return carry
+
+    lax.fori_loop(0, n_section, visit, 0, unroll=4)
 
 
 def per_device(density, momentum, energy, membership, slot_of_brick):
     planes, rows, width = density.shape
     n_section = rows // 4
     block_rows = -(-n_section // 8) * 8
-    shards = CORES * X_CHIPS
+    shards = CORES * Y_CHIPS
     depth = 64 // shards
     f32 = jnp.float32
     height = rows + 2 * EDGE
@@ -615,7 +613,7 @@
             pltpu.VMEM((FIELDS, GROUPS // width, 8, width), f32),
             pltpu.VMEM((shards, depth, width), f32),
             pltpu.VMEM((shards - 1, depth, width), f32),
-            pltpu.VMEM((max(Y_CHIPS - 1, 1), depth, width), f32),
+            pltpu.VMEM((max(X_CHIPS - 1, 1), depth, width), f32),
             pltpu.VMEM((Z_HI * Z_LO - 1, depth, width), f32),
             pltpu.VMEM((3, depth, width), f32),
             pltpu.VMEM((shards, depth, width), f32),
@@ -640,27 +638,16 @@
     )(slot_of_brick, density, momentum, energy, membership, row_matrix(rows), brick_matrix(), depth_matrix(), outer_matrix(rows))
     return pl.pallas_call(
         place_kernel,
-        grid=(FIELDS,),
         out_shape=(
             jax.ShapeDtypeStruct((FIELDS, planes, 4, n_section * width), f32),
             jax.ShapeDtypeStruct((FIELDS, GROUPS), f32),
         ),
-        in_specs=[
-            smem,
-            pl.BlockSpec((64, width), lambda f: (0, 0)),
-            pl.BlockSpec(membership.shape, lambda f: (0, 0)),
-            pl.BlockSpec((n_section, 1, planes, 4, width), lambda f: (0, f, 0, 0, 0)),
-            pl.BlockSpec((n_section, 4, width), lambda f: (0, 0, 0)),
-        ],
-        out_specs=(
-            pl.BlockSpec((1, planes, 4, n_section * width), lambda f: (f, 0, 0, 0)),
-            pl.BlockSpec((FIELDS, GROUPS), lambda f: (0, 0)),
-        ),
+        in_specs=[smem, vmem, vmem, vmem, vmem],
+        out_specs=(vmem, vmem),
         scratch_shapes=[
             pltpu.VMEM((8, GROUPS), f32),
             pltpu.VMEM((FIELDS, n_section, 1, width), f32),
-            pltpu.VMEM((rows, width), f32),
-            pltpu.VMEM((n_section, planes, 4, width), f32),
+            pltpu.VMEM((n_section, FIELDS, planes, 4, width), f32),
         ],
         name="place",
     )(slot_of_brick, final, membership, landed, fringe)

time: 72.4 us -> 70.1 us (0.968)
  the two profiles are of different devices: /device:TPU:14 before, /device:TPU:1 now
where the time goes in v5:
time: 70.1 us; the launch traced here: 69.1 us
  Pallas kernels  68.4 us (98%)
    pallas_call x1, Pallas kernels, per_device(): pl.pallas_call(step_kernel, out_shape=(jax.ShapeDtypeStruct((n_section, F...  64.9 us
    pallas_call x1, Pallas kernels, per_device(): pl.pallas_call(place_kernel, out_shape=(jax.ShapeDtypeStruct((FIELDS, pla...  3.52 us

profile of v5, /device:TPU:1, one launch (start us, length us, event | category | flops | bytes accessed | tf_op | source)
XLA Modules:
  0.0 69.1 jit_solution(10015779388552799203)
XLA Ops:
  0.6 64.9 %step.1 = (f32[24,5,4,4,128]{4,3,2,1,0:T(4,128)}, f32[24,4,128]{2,1,0:T(4,128)}, f32[64,128]{1,0:T(8,128)}) custom-call(s32[1,24]{1,0:T(1,128)} %slot_ref.3, f32[4,96,128]{2,1,0:T(8,128)} %density.1, f32[3,4,96,128]{3,2,1,0:T(8,128)} %momentum.1, f32[4,96,128]{2,1,0:T(8,128)} %energy.1, s32[1,768]{1,0:T(1,128)} %members.3, ...), custom_call_target="tpu_custom_call" | custom-call | tf_op jit(solution)/shard_map/step/pallas_call | solution.py:586
  65.6 3.5 %place.1 = (f32[5,4,4,3072]{3,2,1,0:T(4,128)}, f32[5,1536]{1,0:T(8,128)}) custom-call(s32[1,24]{1,0:T(1,128)} %slot_ref.3, f32[64,128]{1,0:T(8,128)} %get-tuple-element.5.final, s32[1,768]{1,0:T(1,128)} %members.3, f32[24,5,4,4,128]{4,3,2,1,0:T(4,128)} %get-tuple-element.6.landed, f32[24,4,128]{2,1,0:T(4,128)} %get-tuple-element.7.fringe), custom_call_target="tpu_custom_call" | custom-call | tf_op jit(solution)/shard_map/place/pallas_call | solution.py:639

commit v6 on v5

--- a/solution.py
+++ b/solution.py
@@ -320,26 +320,24 @@
             outbox[:, f, k] = plane.reshape(n_section, 4, LANES)
             planes_done[f, k] = plane
 
-        @pl.when(f == 0)
-        def _():
-            pl.semaphore_wait(barrier, greetings)
-            for copy in halo_copies():
-                copy.start()
-
-            def send_small(d, carry):
-                to = (t + d) % n_section
-                send(members, member_rows.at[t], member_send, member_recv, (s, to))
-                send(fringe_out.at[to], fringe.at[t], fringe_send, fringe_recv, (s, to))
-                return carry
-
-            lax.fori_loop(1, n_section, send_small, 0)
-            pltpu.make_async_copy(fringe_out.at[t], fringe.at[t], fringe_own).start()
-
         @pl.when(f == 2)
         def _():
             deliver(0, 3)
 
         return carry
+
+    pl.semaphore_wait(barrier, greetings)
+    for copy in halo_copies():
+        copy.start()
+
+    def send_small(d, carry):
+        to = (t + d) % n_section
+        send(members, member_rows.at[t], member_send, member_recv, (s, to))
+        send(fringe_out.at[to], fringe.at[t], fringe_send, fringe_recv, (s, to))
+        return carry
+
+    lax.fori_loop(1, n_section, send_small, 0)
+    pltpu.make_async_copy(fringe_out.at[t], fringe.at[t], fringe_own).start()
 
     lax.fori_loop(0, FIELDS, early, 0)
 
@@ -465,7 +463,7 @@
                 best[f, col] = top
         return tuple(pltpu.roll(a, LANES - 1, 1) for a in carry)
 
-    lax.fori_loop(0, 32, collect, (labels, *peaks))
+    lax.fori_loop(0, 32, collect, (labels, *peaks), unroll=2)
 
     depth = own.shape[1]
     own[...] = jnp.zeros(own.shape, jnp.float32)

time: 70.1 us -> 69.2 us (0.987)
    pallas_call x1, Pallas kernels: 64.9 us -> 64.2 us  [per_device(): pl.pallas_call(step_kernel, out_shape=(jax.ShapeDtypeStruct((n_section, F...]
where the time goes in v6:
time: 69.2 us; the launch traced here: 68.4 us
  Pallas kernels  67.7 us (98%)
    pallas_call x1, Pallas kernels, per_device(): pl.pallas_call(step_kernel, out_shape=(jax.ShapeDtypeStruct((n_section, F...  64.2 us
    pallas_call x1, Pallas kernels, per_device(): pl.pallas_call(place_kernel, out_shape=(jax.ShapeDtypeStruct((FIELDS, pla...  3.53 us

profile of v6, /device:TPU:1, one launch (start us, length us, event | category | flops | bytes accessed | tf_op | source)
XLA Modules:
  0.0 68.4 jit_solution(8348429704469781931)
XLA Ops:
  0.6 64.2 %step.1 = (f32[24,5,4,4,128]{4,3,2,1,0:T(4,128)}, f32[24,4,128]{2,1,0:T(4,128)}, f32[64,128]{1,0:T(8,128)}) custom-call(s32[1,24]{1,0:T(1,128)} %slot_ref.3, f32[4,96,128]{2,1,0:T(8,128)} %density.1, f32[3,4,96,128]{3,2,1,0:T(8,128)} %momentum.1, f32[4,96,128]{2,1,0:T(8,128)} %energy.1, s32[1,768]{1,0:T(1,128)} %members.3, ...), custom_call_target="tpu_custom_call" | custom-call | tf_op jit(solution)/shard_map/step/pallas_call | solution.py:584
  64.8 3.5 %place.1 = (f32[5,4,4,3072]{3,2,1,0:T(4,128)}, f32[5,1536]{1,0:T(8,128)}) custom-call(s32[1,24]{1,0:T(1,128)} %slot_ref.3, f32[64,128]{1,0:T(8,128)} %get-tuple-element.5.final, s32[1,768]{1,0:T(1,128)} %members.3, f32[24,5,4,4,128]{4,3,2,1,0:T(4,128)} %get-tuple-element.6.landed, f32[24,4,128]{2,1,0:T(4,128)} %get-tuple-element.7.fringe), custom_call_target="tpu_custom_call" | custom-call | tf_op jit(solution)/shard_map/place/pallas_call | solution.py:637
